TPU v7x, 32 devices: a whole 2x2x4 slice. The times are simulated.
32 devices in a mesh: sa: 16 (over z, x, core), sb: 2 (over y).
Axes of the slice: x: 2, y: 2, z: 4, core: 2. Of those that a mesh axis runs over, the one named last changes fastest.
Arguments:
- tokens: bfloat16 [64, 32, 32, 2048], P('sa', 'sb'), may hold values from -6 to 6
- norm_gain: float32 [2048], replicated, may hold values from 0.5 to 1.5
- gate_weight: bfloat16 [2048, 2048], P(('sa', 'sb')), may hold values from -0.125 to 0.125
- level_one: bfloat16 [32, 32, 64, 64], P('sb', 'sa'), may hold values from -0.75 to 0.75
- level_two: bfloat16 [64, 32, 32, 32], P('sa', 'sb'), may hold values from -1 to 1
- level_three: bfloat16 [64, 32, 32, 32], P('sa', 'sb'), may hold values from -1 to 1
- upstream: bfloat16 [64, 32, 32, 2048], P('sa', 'sb'), may hold values from -6 to 6
Outputs:
- output: bfloat16 [64, 32, 32, 2048], P('sa', 'sb')
- grad_tokens: bfloat16 [64, 32, 32, 2048], P('sa', 'sb')
- grad_one: float32 [32, 32, 64, 64], P('sb', 'sa')
- grad_two: float32 [64, 32, 32, 32], P('sa', 'sb')
- grad_three: float32 [64, 32, 32, 32], P('sa', 'sb')
All inputs are finite; a program needn't handle non-finite values.
Results may differ from a plain program's by a relative error of at most 0.0071.
Values may be sent and summed in bfloat16 or wider, within the bound.
No kernel may reach another device: no remote copies, remote signals or barrier semaphores. Data moves between devices by JAX's collectives and lax.ppermute only.
A program may use at most 192 MiB of HBM per device.

v0:
```python
import jax
import jax.numpy as jnp
from jax import lax
from jax.sharding import PartitionSpec as P

EPSILON = 1e-06


def across_first(values, handle):
    return handle(lax.all_to_all(values, "sa", split_axis=2, concat_axis=0, tiled=True))


def return_first(values):
    return lax.all_to_all(values, "sa", split_axis=0, concat_axis=2, tiled=True)


def across_second(values, handle):
    return handle(lax.all_to_all(values, "sb", split_axis=2, concat_axis=1, tiled=True))


def return_second(values):
    return lax.all_to_all(values, "sb", split_axis=1, concat_axis=2, tiled=True)


def body(tokens, norm_gain, gate_weight, level_one, level_two, level_three, upstream):
    channels = tokens.shape[3]
    tokens_float = tokens.astype(jnp.float32)
    inverse_rms = lax.rsqrt(jnp.mean(tokens_float * tokens_float, axis=3, keepdims=True) + EPSILON)
    normed = (tokens_float * inverse_rms * norm_gain).astype(jnp.bfloat16)
    token_rows = normed.reshape(-1, channels)
    gate_pre = jnp.dot(
        token_rows,
        lax.all_gather(gate_weight, ("sa", "sb"), axis=0, tiled=True),
        preferred_element_type=jnp.float32,
    )
    gate_pre = gate_pre.reshape(tokens.shape)

    def first_level(spread):
        blended = jnp.einsum(
            "jkoi,ijkc->ojkc", level_one, spread, preferred_element_type=jnp.float32
        )
        return (return_first(blended.astype(jnp.bfloat16)), spread)

    first_mix, spread_one = across_first(normed, first_level)

    def second_level(spread):
        blended = jnp.einsum(
            "ikoj,ijkc->iokc", level_two, spread, preferred_element_type=jnp.float32
        )
        return (return_second(blended.astype(jnp.bfloat16)), spread)

    second_mix, spread_two = across_second(first_mix, second_level)
    mixed_all = jnp.einsum(
        "ijok,ijkc->ijoc", level_three, second_mix, preferred_element_type=jnp.float32
    )
    gate_sigmoid = jax.nn.sigmoid(gate_pre)
    gate_value = gate_pre * gate_sigmoid
    output = (tokens_float + mixed_all * gate_value).astype(jnp.bfloat16)
    upstream_float = upstream.astype(jnp.float32)
    grad_mixed = (upstream_float * gate_value).astype(jnp.bfloat16)
    grad_gate = (
        upstream_float * mixed_all * gate_sigmoid * (1.0 + gate_pre * (1.0 - gate_sigmoid))
    ).astype(jnp.bfloat16)
    grad_scale = channels ** (-0.5)
    grad_three = (
        jnp.einsum("ijoc,ijkc->ijok", grad_mixed, second_mix, preferred_element_type=jnp.float32)
        * grad_scale
    )
    grad_second = jnp.einsum(
        "ijok,ijoc->ijkc", level_three, grad_mixed, preferred_element_type=jnp.float32
    ).astype(jnp.bfloat16)

    def second_back(spread):
        blended = jnp.einsum(
            "ikoj,iokc->ijkc", level_two, spread, preferred_element_type=jnp.float32
        )
        return (return_second(blended.astype(jnp.bfloat16)), spread)

    grad_first, grad_spread_two = across_second(grad_second, second_back)
    grad_two = (
        jnp.einsum(
            "iokc,ijkc->ikoj", grad_spread_two, spread_two, preferred_element_type=jnp.float32
        )
        * grad_scale
    )

    def first_back(spread):
        blended = jnp.einsum(
            "jkoi,ojkc->ijkc", level_one, spread, preferred_element_type=jnp.float32
        )
        return (return_first(blended.astype(jnp.bfloat16)), spread)

    grad_normed, grad_spread_one = across_first(grad_first, first_back)
    grad_one = (
        jnp.einsum(
            "ojkc,ijkc->jkoi", grad_spread_one, spread_one, preferred_element_type=jnp.float32
        )
        * grad_scale
    )
    grad_rows = grad_gate.reshape(-1, channels)
    back_term = jnp.einsum(
        "tc,rc->tr",
        grad_rows,
        lax.all_gather(gate_weight, ("sa", "sb"), axis=0, tiled=True),
        preferred_element_type=jnp.float32,
    )
    grad_hidden = grad_normed.astype(jnp.float32) + back_term.reshape(tokens.shape)
    weighted = grad_hidden * norm_gain
    average = jnp.mean(weighted * tokens_float, axis=3, keepdims=True)
    grad_tokens = (
        upstream_float + inverse_rms * weighted - tokens_float * inverse_rms**3 * average
    ).astype(jnp.bfloat16)
    return (output, grad_tokens, grad_one, grad_two, grad_three)


def solution(mesh):
    in_specs = (
        P("sa", "sb", None, None),
        P(),
        P(("sa", "sb"), None),
        P("sb", "sa", None, None),
        P("sa", "sb", None, None),
        P("sa", "sb", None, None),
        P("sa", "sb", None, None),
    )
    out_specs = (
        P("sa", "sb", None, None),
        P("sa", "sb", None, None),
        P("sb", "sa", None, None),
        P("sa", "sb", None, None),
        P("sa", "sb", None, None),
    )
    return jax.shard_map(body, mesh=mesh, in_specs=in_specs, out_specs=out_specs, check_vma=False)
```

profile of v0, /device:TPU:11, one launch (start us, length us, event | category | flops | bytes accessed | tf_op | source)
XLA Modules:
  0.0 1615.9 jit_solution(15901734506763919835)
XLA Ops:
  7.2 0.0 copy-start
  7.2 0.0 copy-start.8
  7.2 5.1 fusion.6
  12.3 0.6 multiply_multiply_fusion
  12.9 0.0 copy-start.5
  12.9 0.0 copy-done.8
  12.9 8.7 fusion.8
  21.7 11.4 copy.51
  33.1 188.8 %all_to_all.135 = bf16[4,16,32,2048]{3,1,0,2:T(8,128)(2,1)S(1)} all-to-all(bf16[4,16,32,2048]{3,1,0,2:T(8,128)(2,1)} %copy.51), channel_id=1, replica_groups=mesh['sa'=16,'sb'=2] {'sa'}, dimensions={2} | all-to-all | bytes 16777216 | tf_op jit(solution)/shard_map/all_to_all | solution.py:10
  221.9 17.3 %copy.83 = bf16[4,16,16,2,2048]{4,0,2,3,1:T(4,128)(2,1)} copy(bf16[4,16,16,2,2048]{4,1,0,3,2:T(8,128)(2,1)S(1)} %bitcast.92) | data formatting | bytes 16777216 | tf_op jit(solution)/shard_map/all_to_all | solution.py:10
  239.2 0.0 copy-start.2
  239.2 12.6 all_to_all.101
  251.8 0.0 copy-done.2
  251.8 5.7 convert_bitcast_fusion.4
  257.6 17.3 %copy.53 = bf16[64,16,2,2048]{3,2,1,0:T(2,128)(2,1)} copy(bf16[64,16,2,2048]{3,0,2,1:T(8,128)(2,1)S(1)} %convert_bitcast_fusion.4) | data formatting | bytes 16777216 | tf_op jit(solution)/shard_map/convert_element_type | solution.py:42
  274.8 5.6 all-to-all-start.1
  280.4 0.2 all-gather.2.cloned.1.call-start
  280.7 0.5 all-gather.2.cloned.1.call-update
  281.1 221.1 %all-to-all-done.1 = bf16[64,16,2,2048]{3,2,1,0:T(2,128)(2,1)} async-done(((bf16[64,16,2,2048]{3,2,1,0:T(2,128)(2,1)}), bf16[64,16,2,2048]{3,2,1,0:T(2,128)(2,1)}, u32[]{:S(2)}, u32[]{:S(2)}) %all-to-all-start.1) | async-done | bytes 8388640 | tf_op jit(solution)/shard_map/all_to_all | solution.py:14
  502.2 11.4 copy.54
  513.6 8.4 copy.55
  522.0 8.4 copy.56
  530.5 103.6 %all_to_all.136 = bf16[4,16,32,2048]{3,1,0,2:T(8,128)(2,1)} all-to-all(bf16[4,16,32,2048]{3,1,0,2:T(8,128)(2,1)} %copy.56), channel_id=1, replica_groups=mesh['sa'=16,'sb'=2] {'sb'}, dimensions={2} | all-to-all | bytes 16777216 | tf_op jit(solution)/shard_map/all_to_all | solution.py:18
  634.0 8.5 copy.58
  642.5 0.0 copy-done.4
  642.5 9.1 convert_bitcast_fusion.3
  651.6 11.2 copy.59
  662.9 102.9 %all_to_all.137 = bf16[4,32,16,2048]{3,2,0,1:T(8,128)(2,1)} all-to-all(bf16[4,32,16,2048]{3,2,0,1:T(8,128)(2,1)} %copy.59), channel_id=1, replica_groups=mesh['sa'=16,'sb'=2] {'sb'}, dimensions={1} | all-to-all | bytes 16777216 | tf_op jit(solution)/shard_map/all_to_all | solution.py:22
  765.8 8.3 copy.60
  774.0 0.0 copy-done
  774.0 11.5 fusion.22
  785.5 0.0 copy-done.5
  785.5 34.5 %fusion = (bf16[4,16,32,2048]{3,2,1,0:T(8,128)(2,1)}, bf16[4,16,32,2048]{3,2,1,0:T(8,128)(2,1)}, f32[4,16,32,2048]{3,2,1,0:T(8,128)}) fusion(bf16[4,16,32,2048]{3,2,1,0:T(8,128)(2,1)} %param.13, f32[4,16,2048,32]{2,3,1,0:T(8,128)} %fusion.22, bf16[4,16,32,2048]{3,2,1,0:T(8,128)(2,1)} %param.7, bf16[2048,2048]{1,0:T(8,128)(2,1)} %all-gather.2.cloned.1.call-done, ...), kind=kOutput, calls=%fused_computation.8 | convolution fusion | flops 17242783744 | bytes 75513856 | tf_op jit(solution)/shard_map/dot_general | solution.py:31
  820.0 9.1 convert_bitcast_fusion.2
  829.1 11.2 copy.62
  840.4 101.8 %all_to_all.138 = bf16[4,16,32,2048]{3,1,0,2:T(8,128)(2,1)} all-to-all(bf16[4,16,32,2048]{3,1,0,2:T(8,128)(2,1)} %copy.62), channel_id=1, replica_groups=mesh['sa'=16,'sb'=2] {'sb'}, dimensions={2} | all-to-all | bytes 16777216 | tf_op jit(solution)/shard_map/all_to_all | solution.py:18
  942.2 8.3 copy.63
  950.4 9.0 convert_bitcast_fusion.1
  959.4 11.3 copy.65
  970.8 101.1 %all_to_all.139 = bf16[4,32,16,2048]{3,2,0,1:T(8,128)(2,1)} all-to-all(bf16[4,32,16,2048]{3,2,0,1:T(8,128)(2,1)} %copy.65), channel_id=1, replica_groups=mesh['sa'=16,'sb'=2] {'sb'}, dimensions={1} | all-to-all | bytes 16777216 | tf_op jit(solution)/shard_map/all_to_all | solution.py:22
  1071.9 8.4 copy.67
  1080.3 11.2 copy.68
  1091.5 190.3 %all_to_all.140 = bf16[4,16,32,2048]{3,1,0,2:T(8,128)(2,1)S(1)} all-to-all(bf16[4,16,32,2048]{3,1,0,2:T(8,128)(2,1)} %copy.68), channel_id=1, replica_groups=mesh['sa'=16,'sb'=2] {'sa'}, dimensions={2} | all-to-all | bytes 16777216 | tf_op jit(solution)/shard_map/all_to_all | solution.py:10
  1281.8 17.4 %copy.70 = bf16[16,4,16,2,2048]{4,1,0,3,2:T(4,128)(2,1)} copy(bf16[16,4,16,2,2048]{4,2,1,3,0:T(8,128)(2,1)S(1)} %bitcast.101) | data formatting | bytes 16777216 | tf_op jit(solution)/shard_map/all_to_all | solution.py:10
  1299.2 12.6 all_to_all.125
  1311.8 0.0 copy-done.3
  1311.8 9.0 convert_bitcast_fusion
  1320.7 16.4 %copy.72 = bf16[64,16,2,2048]{3,2,1,0:T(2,128)(2,1)} copy(bf16[64,16,2,2048]{3,0,2,1:T(8,128)(2,1)} %convert_bitcast_fusion) | data formatting | bytes 16777216 | tf_op jit(solution)/shard_map/convert_element_type | solution.py:91
  1337.2 5.9 all-to-all-start.7
  1343.1 0.0 slice-start
  1343.1 9.2 convolution_multiply_fusion
  1352.3 9.2 convolution_multiply_fusion.1
  1361.5 0.0 slice-done
  1361.5 0.0 slice-done.1
  1361.5 7.6 convolution_multiply_fusion.2
  1369.2 156.1 %all-to-all-done.7 = bf16[64,16,2,2048]{3,2,1,0:T(2,128)(2,1)} async-done(((bf16[64,16,2,2048]{3,2,1,0:T(2,128)(2,1)}), bf16[64,16,2,2048]{3,2,1,0:T(2,128)(2,1)}, u32[]{:S(2)}, u32[]{:S(2)}) %all-to-all-start.7) | async-done | bytes 8388640 | tf_op jit(solution)/shard_map/all_to_all | solution.py:14
  1525.3 11.9 copy_bitcast_fusion
  1537.1 20.5 %reshape.41 = f32[4,16,32,2048]{3,2,1,0:T(8,128)} reshape(f32[4,16,16,2,2048]{4,3,2,1,0:T(2,128)} %copy_bitcast_fusion) | data formatting | bytes 33554432 | tf_op jit(solution)/shard_map/convert_element_type | solution.py:107
  1557.6 36.0 %fusion.11 = (f32[4,16,32]{2,1,0:T(8,128)S(1)}, f32[4,16,32,2048]{3,2,1,0:T(8,128)}) fusion(bf16[4,16,32,2048]{3,2,1,0:T(8,128)(2,1)} %param.7, f32[2048]{0:T(1024)S(1)} %copy-done.8, f32[4,16,32,2048]{3,2,1,0:T(8,128)} %reshape.41, bf16[2048,2048]{1,0:T(8,128)(2,1)} %all-gather.2.cloned.1.call-done, bf16[4,16,32,2048]{3,2,1,0:T(8,128)(2,1)} %param.13, ...), kind=kOutput, calls=%fused_computation.19 | convolution fusion | flops 17246976000 | bytes 92291072 | tf_op jit(solution)/shard_map/tc,rc->tr/dot_general | solution.py:101
  1593.6 0.0 copy-done.6
  1593.6 0.0 copy-done.7
  1593.6 0.0 copy-start.1
  1593.7 15.2 fusion.5
  1608.8 0.0 copy-done.1
  (8 shorter events, 0.0 us)
Async XLA Ops:
  7.2 766.9 %copy-start = (bf16[4,16,32,32]{3,2,1,0:T(8,128)(2,1)S(1)}, bf16[4,16,32,32]{3,2,1,0:T(8,128)(2,1)}, u32[]{:S(2)}) copy-start(bf16[4,16,32,32]{3,2,1,0:T(8,128)(2,1)} %param.12) | copy-start | bytes 393220
  7.2 5.8 copy-start.8
  12.9 772.5 %copy-start.5 = (f32[4,16,32]{2,1,0:T(8,128)}, f32[4,16,32]{2,1,0:T(8,128)S(1)}, u32[]{:S(2)}) copy-start(f32[4,16,32]{2,1,0:T(8,128)S(1)} %get-tuple-element.8) | copy-start | bytes 24580
  239.2 12.6 copy-start.2
  274.8 227.4 %all-to-all-start.1 = ((bf16[64,16,2,2048]{3,2,1,0:T(2,128)(2,1)}), bf16[64,16,2,2048]{3,2,1,0:T(2,128)(2,1)}, u32[]{:S(2)}, u32[]{:S(2)}) async-start(bf16[64,16,2,2048]{3,2,1,0:T(2,128)(2,1)} %copy.53), calls=%async_computation.1 | async-start | bytes 16777216 | tf_op jit(solution)/shard_map/all_to_all | solution.py:14
  280.4 505.1 %all-gather.2.cloned.1.call-start = ((), (), s32[]{:S(2)}) async-start(), calls=%async_computation.8 | async-start | bytes 8650752 | tf_op jit(solution)/shard_map/all_gather | solution.py:33
  634.0 8.5 copy-start.4
  1299.2 12.6 copy-start.3
  1337.2 188.1 %all-to-all-start.7 = ((bf16[64,16,2,2048]{3,2,1,0:T(2,128)(2,1)}), bf16[64,16,2,2048]{3,2,1,0:T(2,128)(2,1)}, u32[]{:S(2)}, u32[]{:S(2)}) async-start(bf16[64,16,2,2048]{3,2,1,0:T(2,128)(2,1)} %copy.72), calls=%async_computation.7 | async-start | bytes 16777216 | tf_op jit(solution)/shard_map/all_to_all | solution.py:14
  1343.1 18.5 %slice-start = ((s8[8388608]{0:T(1024)(128)(4,1)}), s8[4194304]{0:T(1024)(128)(4,1)S(1)}, s32[]{:S(2)}) async-start(s8[8388608]{0:T(1024)(128)(4,1)} %bitcast.84), calls=%async_computation.9 | async-start | bytes 8388608
  1352.3 9.2 slice-start.1
  1557.6 36.0 %copy-start.6 = (f32[4,16,32]{2,1,0:T(8,128)S(1)}, f32[4,16,32]{2,1,0:T(8,128)}, u32[]{:S(2)}) copy-start(f32[4,16,32]{2,1,0:T(8,128)} %copy-done.5) | copy-start | bytes 24580
  1557.6 36.0 %copy-start.7 = (f32[4,16,32]{2,1,0:T(8,128)S(1)}, f32[4,16,32]{2,1,0:T(8,128)}, u32[]{:S(2)}) copy-start(f32[4,16,32]{2,1,0:T(8,128)} %get-tuple-element.7) | copy-start | bytes 24580
  1593.6 15.2 copy-start.1
Sparse Core Ops, SparseCore 0:
  284.3 184.3 all-gather.1
where the time goes:
time: 1630 us; the launch traced here: 1620 us
  blocking collectives  788 us (48%)
  waiting for transfers between devices  378 us (23%)
  local copies, waits for them, and re-layouts  232 us (14%)
  matrix products  150 us (9%)
  other arithmetic  41.5 us (3%)
    all_to_all x2, blocking collectives, across_first(): lax.all_to_all(values, 'sa', split_axis=2, concat_axis=0, tiled=True)  379 us
    all_to_all x2, waiting for transfers between devices, return_first(): return lax.all_to_all(values, 'sa', split_axis=0, concat_axis=2, tiled=True)  377 us
    all_to_all x2, blocking collectives, across_second(): lax.all_to_all(values, 'sb', split_axis=2, concat_axis=1, tiled=True)  205 us
    all_to_all x2, blocking collectives, return_second(): return lax.all_to_all(values, 'sb', split_axis=1, concat_axis=2, tiled=True)  204 us
    all_to_all x4, local copies, waits for them, and re-layouts, across_first(): lax.all_to_all(values, 'sa', split_axis=2, concat_axis=0, tiled=True)  59.9 us
    dot_general x1, matrix products, body(): jnp.einsum('tc,rc->tr', grad_rows, lax.all_gather(gate_weight, ('sa', 'sb...  36 us
    dot_general x1, matrix products, body(): jnp.dot(token_rows, lax.all_gather(gate_weight, ('sa', 'sb'), axis=0, til...  34.5 us
  transfers between devices with their start and end apart: 3, of which 2 were waited for; matrix products, arithmetic and copies ran while one was open for 6% of the time, Pallas kernels for 0%

commit v1 on v0

v1 whole, which is shorter than its diff:
```python
import functools

import jax
import jax.numpy as jnp
from jax import lax
from jax.experimental import pallas as pl
from jax.experimental.pallas import tpu as pltpu
from jax.sharding import PartitionSpec as P

EPSILON = 1e-06
F32 = jnp.float32
BF16 = jnp.bfloat16
CHUNKS = 4
LIMIT = 60 * 1024 * 1024


def dot(left, right):
    return jnp.dot(left, right, preferred_element_type=F32)


def dot_last(left, right):
    return lax.dot_general(left, right, (((1,), (1,)), ((), ())), preferred_element_type=F32)


def position(shape, axis, inner, extent):
    return (lax.broadcasted_iota(jnp.int32, shape, axis) // inner) % extent


def widen(rows, inner, extent, lanes):
    batch, count, width = rows.shape
    wide = width * extent
    source = lax.broadcasted_iota(jnp.int32, (width, wide), 0)
    column = lax.broadcasted_iota(jnp.int32, (width, wide), 1)
    pick = (source == (column // (extent * lanes)) * lanes + column % lanes).astype(BF16)
    full = jnp.einsum("brq,qw->brw", rows, pick, preferred_element_type=F32)
    keep = position((count, wide), 0, inner, extent) == position((count, wide), 1, lanes, extent)
    return jnp.where(keep[None], full, 0.0).astype(BF16)


def fold(total, inner, extent, lanes):
    count, wide = total.shape
    width = wide // extent
    keep = position((count, wide), 0, inner, extent) == position((count, wide), 1, lanes, extent)
    source = lax.broadcasted_iota(jnp.int32, (wide, width), 1)
    column = lax.broadcasted_iota(jnp.int32, (wide, width), 0)
    pick = (source == (column // (extent * lanes)) * lanes + column % lanes).astype(F32)
    return jnp.dot(
        jnp.where(keep, total, 0.0), pick, precision=lax.Precision.HIGHEST, preferred_element_type=F32
    )


def params(count):
    return pltpu.CompilerParams(
        dimension_semantics=("arbitrary",) * count, vmem_limit_bytes=LIMIT
    )


def cost(flops, moved):
    return pl.CostEstimate(flops=int(flops), bytes_accessed=int(moved), transcendentals=0)


def first_kernel(matrix, values, out):
    shape = out.shape
    flat = values[...].reshape(-1, shape[3])
    out[...] = dot(matrix[0], flat).astype(BF16).reshape(shape)


def first_level(matrix, values):
    away, low, rows, width = values.shape
    if rows % 16:
        flat = values.transpose(1, 0, 2, 3).reshape(low, away * rows, width)
        mixed = jnp.einsum("krs,ksc->krc", matrix, flat, preferred_element_type=F32).astype(BF16)
        return mixed.reshape(low, away, rows, width).transpose(1, 0, 2, 3)
    size = away * rows
    spec = pl.BlockSpec((away, 1, rows, width), lambda k: (0, k, 0, 0))
    return pl.pallas_call(
        first_kernel,
        grid=(low,),
        in_specs=[pl.BlockSpec((1, size, size), lambda k: (k, 0, 0)), spec],
        out_specs=spec,
        out_shape=jax.ShapeDtypeStruct(values.shape, BF16),
        compiler_params=params(1),
        cost_estimate=cost(2 * low * size * size * width, 4 * values.size + 2 * matrix.size),
        name="first",
    )(matrix, values)


def first_back_kernel(lanes, matrix, values, grads, out, total):
    shape = out.shape
    flat = values[...].reshape(-1, shape[3])
    grad = grads[...].reshape(-1, shape[3])
    out[...] = dot(matrix[0], grad).astype(BF16).reshape(shape)
    total[0] = fold(dot_last(grad, flat), 1, lanes, 1)


def first_back(matrix, values, grads, lanes):
    away, low, rows, width = values.shape
    size = away * rows
    if rows % 16:
        flat = values.transpose(1, 0, 2, 3).reshape(low, size, width)
        grad = grads.transpose(1, 0, 2, 3).reshape(low, size, width)
        mixed = jnp.einsum("krs,ksc->krc", matrix, grad, preferred_element_type=F32).astype(BF16)
        full = jnp.einsum("krc,ksc->krs", grad, flat, preferred_element_type=F32)
        total = jnp.stack([fold(full[k], 1, lanes, 1) for k in range(low)])
        return (mixed.reshape(low, away, rows, width).transpose(1, 0, 2, 3), total)
    spec = pl.BlockSpec((away, 1, rows, width), lambda k: (0, k, 0, 0))
    return pl.pallas_call(
        functools.partial(first_back_kernel, lanes),
        grid=(low,),
        in_specs=[pl.BlockSpec((1, size, size), lambda k: (k, 0, 0)), spec, spec],
        out_specs=(spec, pl.BlockSpec((1, size, size // lanes), lambda k: (k, 0, 0))),
        out_shape=(
            jax.ShapeDtypeStruct(values.shape, BF16),
            jax.ShapeDtypeStruct((low, size, size // lanes), F32),
        ),
        compiler_params=params(1),
        cost_estimate=cost(4 * low * size * size * width, 6 * values.size + 2 * matrix.size),
        name="first_back",
    )(matrix, values, grads)


def second_kernel(parts, matrix, *refs):
    ins, outs = refs[:parts], refs[parts:]
    rows = outs[0].shape[1]
    for k in range(matrix.shape[0]):
        flat = jnp.concatenate([ref[k] for ref in ins], axis=0)
        mixed = dot(matrix[k], flat).astype(BF16)
        for part in range(parts):
            outs[part][k] = mixed[part * rows : (part + 1) * rows]


def second_level(matrix, pieces):
    parts = len(pieces)
    count, rows, width = pieces[0].shape
    if rows % 16:
        flat = jnp.concatenate(pieces, axis=1)
        mixed = jnp.einsum("krs,ksc->krc", matrix, flat, preferred_element_type=F32).astype(BF16)
        return tuple(jnp.split(mixed, parts, axis=1))
    step = 4 if count % 4 == 0 else 1
    size = parts * rows
    spec = pl.BlockSpec((step, rows, width), lambda k: (k, 0, 0))
    return pl.pallas_call(
        functools.partial(second_kernel, parts),
        grid=(count // step,),
        in_specs=[pl.BlockSpec((step, size, size), lambda k: (k, 0, 0))] + [spec] * parts,
        out_specs=(spec,) * parts,
        out_shape=(jax.ShapeDtypeStruct(pieces[0].shape, BF16),) * parts,
        compiler_params=params(1),
        cost_estimate=cost(2 * count * size * size * width, 4 * parts * pieces[0].size),
        name="second",
    )(matrix, *pieces)


def second_back_kernel(parts, inner, lanes, matrix, *refs):
    grads, values = refs[:parts], refs[parts : 2 * parts]
    outs, total = refs[2 * parts : 3 * parts], refs[3 * parts]
    rows = outs[0].shape[1]
    for k in range(matrix.shape[0]):
        grad = jnp.concatenate([ref[k] for ref in grads], axis=0)
        flat = jnp.concatenate([ref[k] for ref in values], axis=0)
        mixed = dot(matrix[k], grad).astype(BF16)
        for part in range(parts):
            outs[part][k] = mixed[part * rows : (part + 1) * rows]
        total[k] = fold(dot_last(grad, flat), inner, lanes, inner)


def second_back(matrix, grads, values, inner, lanes):
    parts = len(grads)
    count, rows, width = grads[0].shape
    size = parts * rows
    if rows % 16:
        grad = jnp.concatenate(grads, axis=1)
        flat = jnp.concatenate(values, axis=1)
        mixed = jnp.einsum("krs,ksc->krc", matrix, grad, preferred_element_type=F32).astype(BF16)
        full = jnp.einsum("krc,ksc->krs", grad, flat, preferred_element_type=F32)
        total = jnp.stack([fold(full[k], inner, lanes, inner) for k in range(count)])
        return (tuple(jnp.split(mixed, parts, axis=1)), total)
    step = 4 if count % 4 == 0 else 1
    spec = pl.BlockSpec((step, rows, width), lambda k: (k, 0, 0))
    result = pl.pallas_call(
        functools.partial(second_back_kernel, parts, inner, lanes),
        grid=(count // step,),
        in_specs=[pl.BlockSpec((step, size, size), lambda k: (k, 0, 0))] + [spec] * (2 * parts),
        out_specs=(spec,) * parts
        + (pl.BlockSpec((step, size, size // lanes), lambda k: (k, 0, 0)),),
        out_shape=(jax.ShapeDtypeStruct(grads[0].shape, BF16),) * parts
        + (jax.ShapeDtypeStruct((count, size, size // lanes), F32),),
        compiler_params=params(1),
        cost_estimate=cost(4 * count * size * size * width, 6 * parts * grads[0].size),
        name="second_back",
    )(matrix, *grads, *values)
    return (result[:parts], result[parts])


def gate_math(mixed, gate_pre, tokens, upstream):
    gate_sigmoid = jax.nn.sigmoid(gate_pre)
    gate_value = gate_pre * gate_sigmoid
    output = (tokens.astype(F32) + mixed * gate_value).astype(BF16)
    upstream = upstream.astype(F32)
    grad_mixed = (upstream * gate_value).astype(BF16)
    grad_gate = (
        upstream * mixed * gate_sigmoid * (1.0 + gate_pre * (1.0 - gate_sigmoid))
    ).astype(BF16)
    return (output, grad_mixed, grad_gate)


def third_kernel(parts, lanes, matrix, matrix_back, gate_pre, tokens, upstream, *refs):
    ins = refs[:parts]
    output, grad_gate = refs[parts], refs[parts + 1]
    outs, total = refs[parts + 2 : 2 * parts + 2], refs[2 * parts + 2]
    shape = output.shape
    width = shape[3]
    flat = jnp.concatenate([ref[...].reshape(-1, width) for ref in ins], axis=0)
    mixed = dot(matrix[0], flat)
    result, grad_mixed, gate_grad = gate_math(
        mixed,
        gate_pre[...].reshape(-1, width),
        tokens[...].reshape(-1, width),
        upstream[...].reshape(-1, width),
    )
    output[...] = result.reshape(shape)
    grad_gate[...] = gate_grad.reshape(shape)
    back = dot(matrix_back[0], grad_mixed).astype(BF16)
    rows = back.shape[0] // parts
    for part in range(parts):
        outs[part][...] = back[part * rows : (part + 1) * rows].reshape(outs[part].shape)
    total[0] = fold(dot_last(grad_mixed, flat), 1, lanes, 1)


def third_level(matrix, matrix_back, gate_pre, tokens, upstream, offset, pieces):
    parts = len(pieces)
    low, heads, lanes, width = pieces[0].shape
    count = low * parts
    size = count * lanes
    if lanes % 16:
        flat = jnp.concatenate(pieces, axis=0).transpose(1, 0, 2, 3).reshape(heads, size, width)
        mixed = jnp.einsum("irs,isc->irc", matrix, flat, preferred_element_type=F32)

        def turn(value):
            return value.reshape(heads, count, lanes, width).transpose(1, 0, 2, 3)

        def local(value):
            value = lax.slice_in_dim(value, offset * width, (offset + 1) * width, axis=3)
            return value.transpose(1, 0, 2, 3).reshape(heads, size, width)

        pre = gate_pre.transpose(1, 0, 2, 3).reshape(heads, size, width)
        result, grad_mixed, gate_grad = gate_math(mixed, pre, local(tokens), local(upstream))
        back = jnp.einsum("irs,isc->irc", matrix_back, grad_mixed, preferred_element_type=F32)
        full = jnp.einsum("irc,isc->irs", grad_mixed, flat, preferred_element_type=F32)
        total = jnp.stack([fold(full[i], 1, lanes, 1) for i in range(heads)])
        outs = tuple(jnp.split(turn(back.astype(BF16)), parts, axis=0))
        return (turn(result), turn(gate_grad), outs, total)
    whole = pl.BlockSpec((count, 1, lanes, width), lambda i: (0, i, 0, 0))
    shifted = pl.BlockSpec((count, 1, lanes, width), lambda i: (0, i, 0, offset))
    part = pl.BlockSpec((low, 1, lanes, width), lambda i: (0, i, 0, 0))
    square = pl.BlockSpec((1, size, size), lambda i: (i, 0, 0))
    full = jax.ShapeDtypeStruct((count, heads, lanes, width), BF16)
    result = pl.pallas_call(
        functools.partial(third_kernel, parts, lanes),
        grid=(heads,),
        in_specs=[square, square, whole, shifted, shifted] + [part] * parts,
        out_specs=(whole, whole)
        + (part,) * parts
        + (pl.BlockSpec((1, size, count), lambda i: (i, 0, 0)),),
        out_shape=(full, full)
        + (jax.ShapeDtypeStruct(pieces[0].shape, BF16),) * parts
        + (jax.ShapeDtypeStruct((heads, size, count), F32),),
        compiler_params=params(1),
        cost_estimate=cost(6 * heads * size * size * width, 18 * heads * size * width),
        name="third",
    )(matrix, matrix_back, gate_pre, tokens, upstream, *pieces)
    return (result[0], result[1], result[2 : parts + 2], result[parts + 2])


def ahead(values, axis, me, count):
    doubled = jnp.concatenate([values, values], axis=axis)
    return lax.dynamic_slice_in_dim(doubled, me, count, axis=axis)


def behind(values, axis, me, count):
    return ahead(jnp.flip(values, axis=axis), axis, count - 1 - me, count)


def exchange(blocks):
    count = len(blocks)
    return [blocks[0]] + [
        lax.ppermute(blocks[r], "sb", [(n, (n + r) % count) for n in range(count)])
        for r in range(1, count)
    ]


def across_first(values):
    return lax.all_to_all(values, "sa", split_axis=0, concat_axis=0, tiled=True)


def body(parts, away, tokens, norm_gain, gate_weight, level_one, level_two, level_three, upstream):
    heads, lanes, thirds, channels = tokens.shape
    firsts = level_one.shape[2]
    low = thirds // away
    near = thirds // parts
    me = lax.axis_index("sb")
    width = channels // CHUNKS
    rows = heads * lanes

    tokens_float = tokens.astype(F32)
    inverse_rms = lax.rsqrt(jnp.mean(tokens_float * tokens_float, axis=3, keepdims=True) + EPSILON)

    def normalised(values, scale, gain):
        return (values.astype(F32) * scale * gain).astype(BF16)

    spreads = []
    for n in range(CHUNKS):
        at = slice(n * width, (n + 1) * width)
        part = normalised(tokens[..., at], inverse_rms, norm_gain[at])
        part = part.transpose(2, 0, 1, 3).reshape(away, low, rows, width)
        spreads.append(across_first(part))

    weight = lax.all_gather(gate_weight, ("sa", "sb"), axis=0, tiled=True)
    one = level_one.transpose(1, 2, 0, 3).reshape(low, firsts * lanes, firsts)
    one_back = level_one.transpose(1, 3, 0, 2).reshape(low, firsts * lanes, firsts)
    matrix_one = widen(one, 1, lanes, 1)
    matrix_one_back = widen(one_back, 1, lanes, 1)

    two = level_two.reshape(heads, near, parts, lanes, parts, lanes)
    two_front = behind(ahead(two, 2, me, parts), 4, me, parts)
    two_back = ahead(behind(two, 2, me, parts), 4, me, parts)
    two_front = two_front.transpose(1, 2, 0, 3, 4, 5).reshape(near, parts * rows, parts * lanes)
    two_back = two_back.transpose(1, 4, 0, 5, 2, 3).reshape(near, parts * rows, parts * lanes)
    matrix_two = widen(two_front, lanes, heads, lanes)
    matrix_two_back = widen(two_back, lanes, heads, lanes)

    three = level_three.reshape(heads, lanes, thirds, parts, near)
    three_front = behind(three, 3, me, parts).reshape(level_three.shape)
    three_back = ahead(three, 3, me, parts).reshape(level_three.shape)
    three_front = three_front.transpose(0, 2, 1, 3).reshape(heads, thirds * lanes, thirds)
    three_back = three_back.transpose(0, 3, 1, 2).reshape(heads, thirds * lanes, thirds)
    matrix_three = widen(three_front, 1, lanes, 1)
    matrix_three_back = widen(three_back, 1, lanes, 1)

    turned = tokens.transpose(2, 0, 1, 3)
    turned_up = upstream.transpose(2, 0, 1, 3)
    turned_rms = inverse_rms.transpose(2, 0, 1, 3)
    token_rows = normalised(turned, turned_rms, norm_gain).reshape(-1, channels)

    def half(values, n):
        return lax.dynamic_slice_in_dim(values, n * near, near, axis=0)

    outputs, gate_grads, normed_grads = [], [], []
    total_one = total_two = total_three = 0.0
    for n in range(CHUNKS):
        at = slice(n * width, (n + 1) * width)
        mixed = across_first(first_level(matrix_one, spreads[n]))
        mixed = mixed.reshape(thirds, rows, width)
        spread_two = exchange([half(mixed, (me + r) % parts) for r in range(parts)])
        second = exchange(list(second_level(matrix_two, spread_two)))
        second = [piece.reshape(near, heads, lanes, width) for piece in second]
        gate_pre = dot(token_rows, weight[:, at]).reshape(thirds, heads, lanes, width)
        output, gate_grad, grads, total = third_level(
            matrix_three, matrix_three_back, gate_pre, turned, turned_up, n, second
        )
        outputs.append(output)
        gate_grads.append(gate_grad)
        total_three = total_three + total
        grads = exchange([grad.reshape(near, rows, width) for grad in grads])
        grads, total = second_back(matrix_two_back, grads, spread_two, lanes, heads)
        total_two = total_two + total
        pieces = exchange(list(grads))
        joined = jnp.zeros((thirds, rows, width), BF16)
        for r in range(parts):
            place = ((me - r) % parts) * near
            joined = lax.dynamic_update_slice_in_dim(joined, pieces[r], place, axis=0)
        grads = across_first(joined.reshape(away, low, rows, width))
        grads, total = first_back(matrix_one_back, spreads[n], grads, lanes)
        total_one = total_one + total
        normed_grads.append(across_first(grads).reshape(thirds * rows, width))

    output = jnp.concatenate(outputs, axis=3).transpose(1, 2, 0, 3)
    grad_rows = jnp.concatenate(gate_grads, axis=3).reshape(-1, channels)
    back_term = jnp.einsum("tc,rc->tr", grad_rows, weight, preferred_element_type=F32)
    grad_hidden = jnp.concatenate(normed_grads, axis=1).astype(F32) + back_term
    weighted = grad_hidden.reshape(turned.shape) * norm_gain
    turned_float = turned.astype(F32)
    average = jnp.mean(weighted * turned_float, axis=3, keepdims=True)
    grad_tokens = (
        turned_up.astype(F32) + turned_rms * weighted - turned_float * turned_rms**3 * average
    ).astype(BF16)
    grad_tokens = grad_tokens.transpose(1, 2, 0, 3)

    scale = channels ** (-0.5)
    grad_one = total_one.reshape(low, firsts, lanes, firsts).transpose(2, 0, 1, 3) * scale
    grad_two = total_two.reshape(near, parts, heads, lanes, parts, lanes)
    grad_two = behind(behind(grad_two, 1, me, parts), 4, me, parts)
    grad_two = grad_two.transpose(2, 0, 1, 3, 4, 5).reshape(level_two.shape) * scale
    grad_three = total_three.reshape(heads, thirds, lanes, parts, near)
    grad_three = behind(grad_three, 3, me, parts).reshape(heads, thirds, lanes, thirds)
    grad_three = grad_three.transpose(0, 2, 1, 3) * scale
    return (output, grad_tokens, grad_one, grad_two, grad_three)


def solution(mesh):
    in_specs = (
        P("sa", "sb", None, None),
        P(),
        P(("sa", "sb"), None),
        P("sb", "sa", None, None),
        P("sa", "sb", None, None),
        P("sa", "sb", None, None),
        P("sa", "sb", None, None),
    )
    out_specs = (
        P("sa", "sb", None, None),
        P("sa", "sb", None, None),
        P("sb", "sa", None, None),
        P("sa", "sb", None, None),
        P("sa", "sb", None, None),
    )
    return jax.shard_map(
        functools.partial(body, mesh.shape["sb"], mesh.shape["sa"]),
        mesh=mesh,
        in_specs=in_specs,
        out_specs=out_specs,
        check_vma=False,
    )
```

time: 1630 us -> 1260 us (0.77)
  blocking collectives: 788 us -> 0 us
  Pallas kernels: 0 us -> 214 us
  waiting for transfers between devices: 378 us -> 563 us
  starting transfers between devices: 11.8 us -> 135 us
  local copies, waits for them, and re-layouts: 232 us -> 140 us
  matrix products: 150 us -> 93.4 us
  other arithmetic: 41.5 us -> 89.6 us
    all_to_all x6 -> x0, blocking collectives: 788 us -> none  [the longest x2 379 us: across_first(): lax.all_to_all(values, 'sa', split_axis=2, concat_axis=0, tiled=True)]
    pallas_call x0 -> x20, Pallas kernels: none -> 214 us  [the longest x4 78.4 us: first_back(): pl.pallas_call(functools.partial(first_back_kernel, lanes), grid=(low,),...]
    ppermute x0 -> x16, waiting for transfers between devices: none -> 168 us  [exchange(): lax.ppermute(blocks[r], 'sb', [(n, (n + r) % count) for n in range(count)])]
    all_to_all x12 -> x0, local copies, waits for them, and re-layouts: 133 us -> none  [the longest x4 59.9 us: across_first(): lax.all_to_all(values, 'sa', split_axis=2, concat_axis=0, tiled=True)]
    all_to_all x2 -> x16, starting transfers between devices: 11.5 us -> 129 us  [across_first(): return lax.all_to_all(values, 'sa', split_axis=0, concat_axis=0, tiled=True)]
    convert_element_type x7 -> x0, local copies, waits for them, and re-layouts: 99.4 us -> none  [the longest x1 20.5 us: body(): grad_normed.astype(jnp.float32) + back_term.reshape(tokens.shape)]
    dot_general x11, matrix products: 150 us -> 93.4 us  [the longest x4 52.7 us: dot(): return jnp.dot(left, right, preferred_element_type=F32)]
    unnamed x22 -> x112, local copies, waits for them, and re-layouts: 0.05 us -> 43.1 us
  transfers between devices with their start and end apart: 3 -> 33, of which waited for: 2 -> 24; matrix products, arithmetic and copies ran while one was open for 6% -> 18% of each run, Pallas kernels for 0% -> 17%
where the time goes in v1:
time: 1260 us; the launch traced here: 1250 us
  waiting for transfers between devices  563 us (45%)
  Pallas kernels  214 us (17%)
  local copies, waits for them, and re-layouts  140 us (11%)
  starting transfers between devices  135 us (11%)
  matrix products  93.4 us (7%)
  other arithmetic  89.6 us (7%)
  between operations  15 us (1%)
    all_to_all x16, waiting for transfers between devices, across_first(): return lax.all_to_all(values, 'sa', split_axis=0, concat_axis=0, tiled=True)  395 us
    ppermute x16, waiting for transfers between devices, exchange(): lax.ppermute(blocks[r], 'sb', [(n, (n + r) % count) for n in range(count)])  168 us
    all_to_all x16, starting transfers between devices, across_first(): return lax.all_to_all(values, 'sa', split_axis=0, concat_axis=0, tiled=True)  129 us
    pallas_call x4, Pallas kernels, first_back(): pl.pallas_call(functools.partial(first_back_kernel, lanes), grid=(low,),...  78.4 us
    pallas_call x4, Pallas kernels, third_level(): pl.pallas_call(functools.partial(third_kernel, parts, lanes), grid=(heads...  66.4 us
    dot_general x4, matrix products, dot(): return jnp.dot(left, right, preferred_element_type=F32)  52.7 us
    unnamed x112, local copies, waits for them, and re-layouts  43.1 us
    pallas_call x4, Pallas kernels, second_back(): pl.pallas_call(functools.partial(second_back_kernel, parts, inner, lanes)...  30 us
  transfers between devices with their start and end apart: 33, of which 24 were waited for; matrix products, arithmetic and copies ran while one was open for 18% of the time, Pallas kernels for 17%

profile of v1, /device:TPU:11, one launch (start us, length us, event | category | flops | bytes accessed | tf_op | source)
XLA Modules:
  0.0 1249.8 jit_solution(3926725730152089714)
XLA Ops:
  7.9 5.2 multiply_reduce_fusion
  20.0 6.5 all-to-all-start
  30.6 43.3 %all-to-all-done.values = bf16[16,2,64,512]{3,2,1,0:T(8,128)(2,1)S(1)} async-done(((bf16[16,2,64,512]{3,2,1,0:T(8,128)(2,1)}), bf16[16,2,64,512]{3,2,1,0:T(8,128)(2,1)S(1)}, u32[]{:S(2)}, u32[]{:S(2)}) %all-to-all-start) | async-done | bytes 2097184 | tf_op jit(solution)/shard_map/all_to_all | solution.py:293
  84.1 43.3 %all-to-all-done.2.values = bf16[16,2,64,512]{3,2,1,0:T(8,128)(2,1)S(1)} async-done(((bf16[16,2,64,512]{3,2,1,0:T(8,128)(2,1)}), bf16[16,2,64,512]{3,2,1,0:T(8,128)(2,1)S(1)}, u32[]{:S(2)}, u32[]{:S(2)}) %all-to-all-start.2) | async-done | bytes 2097184 | tf_op jit(solution)/shard_map/all_to_all | solution.py:293
  138.4 59.3 %all-to-all-done.4.values = bf16[16,2,64,512]{3,2,1,0:T(8,128)(2,1)S(1)} async-done(((bf16[16,2,64,512]{3,2,1,0:T(8,128)(2,1)}), bf16[16,2,64,512]{3,2,1,0:T(8,128)(2,1)S(1)}, u32[]{:S(2)}, u32[]{:S(2)}) %all-to-all-start.4) | async-done | bytes 2097184 | tf_op jit(solution)/shard_map/all_to_all | solution.py:293
  197.8 5.4 all-to-all-start.6
  208.6 5.3 first.4
  213.9 58.8 %all-to-all-done.6.values = bf16[16,2,64,512]{3,2,1,0:T(8,128)(2,1)} async-done(((bf16[16,2,64,512]{3,2,1,0:T(8,128)(2,1)}), bf16[16,2,64,512]{3,2,1,0:T(8,128)(2,1)}, u32[]{:S(2)}, u32[]{:S(2)}) %all-to-all-start.6) | async-done | bytes 2097184 | tf_op jit(solution)/shard_map/all_to_all | solution.py:293
  272.7 4.9 all-to-all-start.1
  277.6 5.3 first.5
  283.0 42.1 %all-to-all-done.1 = bf16[16,2,64,512]{3,2,1,0:T(8,128)(2,1)S(1)} async-done(((bf16[16,2,64,512]{3,2,1,0:T(8,128)(2,1)}), bf16[16,2,64,512]{3,2,1,0:T(8,128)(2,1)S(1)}, u32[]{:S(2)}, u32[]{:S(2)}) %all-to-all-start.1) | async-done | bytes 2097184 | tf_op jit(solution)/shard_map/all_to_all | solution.py:293
  331.2 5.4 first.6
  336.5 42.1 %all-to-all-done.3 = bf16[16,2,64,512]{3,2,1,0:T(8,128)(2,1)S(1)} async-done(((bf16[16,2,64,512]{3,2,1,0:T(8,128)(2,1)}), bf16[16,2,64,512]{3,2,1,0:T(8,128)(2,1)S(1)}, u32[]{:S(2)}, u32[]{:S(2)}) %all-to-all-start.3) | async-done | bytes 2097184 | tf_op jit(solution)/shard_map/all_to_all | solution.py:293
  410.2 18.4 %copy_bitcast_fusion = (bf16[32,4,16,2048]{3,2,1,0:T(8,128)(2,1)}, bf16[32,4,16,2048]{3,2,1,0:T(8,128)(2,1)}) fusion(bf16[4,16,32,2048]{3,2,1,0:T(8,128)(2,1)} %param.13, bf16[4,16,32,2048]{3,2,1,0:T(8,128)(2,1)} %param.7), kind=kLoop, calls=%fused_computation.18 | loop fusion | bytes 33554432 | tf_op jit(solution)/shard_map/transpose | solution.py:341
  443.2 5.3 first.7
  448.6 6.3 all-to-all-start.7
  460.6 13.2 %fusion.22.gate_pre = f32[32,4,16,512]{3,2,1,0:T(8,128)} fusion(f32[2048]{0:T(1024)S(1)} %copy-done.38, f32[32,4,16]{2,1,0:T(4,128)S(1)} %copy.122, bf16[2048,2048]{1,0:T(8,128)(2,1)} %all-gather.2.cloned.1.call-done, bf16[4,16,32,2048]{3,2,1,0:T(8,128)(2,1)} %param.7), kind=kOutput, calls=%fused_computation.44 | convolution fusion | flops 4311744512 | bytes 14696448 | tf_op jit(solution)/shard_map/dot_general | solution.py:18
  473.8 11.4 collective-permute-done.1
  485.2 16.7 %third.4 = (bf16[32,4,16,512]{3,2,1,0:T(8,128)(2,1)}, bf16[32,4,16,512]{3,2,1,0:T(8,128)(2,1)}, bf16[16,4,16,512]{3,2,1,0:T(8,128)(2,1)}, bf16[16,4,16,512]{3,2,1,0:T(8,128)(2,1)}, f32[4,512,32]{2,1,0:T(8,128)}) custom-call(bf16[4,512,512]{2,1,0:T(8,128)(2,1)} %select_convert_fusion.1.matrix, bf16[4,512,512]{2,1,0:T(8,128)(2,1)} %select_convert_fusion.matrix_back, ...), custom_call_target="tpu_custom_call" | custom-call | flops 3221225472 | bytes 18874368 | tf_op jit(solution)/shard_map/third/pallas_call | solution.py:258
  511.0 14.7 %collective-permute-done.8.refs_1_ = bf16[16,64,512]{2,1,0:T(8,128)(2,1)} collective-permute-done((bf16[16,64,512]{2,1,0:T(8,128)(2,1)}, bf16[16,64,512]{2,1,0:T(8,128)(2,1)}, u32[]{:S(2)}, u32[]{:S(2)}) %collective-permute-start.8) | collective-permute-done | bytes 1048608 | tf_op jit(solution)/shard_map/ppermute | solution.py:287
  525.7 7.5 second_back.4
  541.7 14.5 %collective-permute-done.9 = bf16[16,64,512]{2,1,0:T(8,128)(2,1)} collective-permute-done((bf16[16,64,512]{2,1,0:T(8,128)(2,1)}, bf16[16,64,512]{2,1,0:T(8,128)(2,1)}, u32[]{:S(2)}, u32[]{:S(2)}) %collective-permute-start.9) | collective-permute-done | bytes 1048608 | tf_op jit(solution)/shard_map/ppermute | solution.py:287
  558.5 11.7 all-to-all-start.8
  570.2 8.5 collective-permute-done.2.refs_1_.refs_3_
  584.0 13.2 %fusion.20.gate_pre = f32[32,4,16,512]{3,2,1,0:T(8,128)} fusion(f32[2048]{0:T(1024)S(1)} %copy-done.38, f32[32,4,16]{2,1,0:T(4,128)S(1)} %copy.122, bf16[2048,2048]{1,0:T(8,128)(2,1)} %all-gather.2.cloned.1.call-done, bf16[4,16,32,2048]{3,2,1,0:T(8,128)(2,1)} %param.7), kind=kOutput, calls=%fused_computation.43 | convolution fusion | flops 4311744512 | bytes 14696448 | tf_op jit(solution)/shard_map/dot_general | solution.py:18
  597.2 9.0 collective-permute-done.3
  607.1 16.6 %third.5 = (bf16[32,4,16,512]{3,2,1,0:T(8,128)(2,1)}, bf16[32,4,16,512]{3,2,1,0:T(8,128)(2,1)}, bf16[16,4,16,512]{3,2,1,0:T(8,128)(2,1)}, bf16[16,4,16,512]{3,2,1,0:T(8,128)(2,1)}, f32[4,512,32]{2,1,0:T(8,128)}) custom-call(bf16[4,512,512]{2,1,0:T(8,128)(2,1)} %select_convert_fusion.1.matrix, bf16[4,512,512]{2,1,0:T(8,128)(2,1)} %select_convert_fusion.matrix_back, ...), custom_call_target="tpu_custom_call" | custom-call | flops 3221225472 | bytes 18874368 | tf_op jit(solution)/shard_map/third/pallas_call | solution.py:258
  623.7 21.3 %collective-permute-done.10.refs_1_ = bf16[16,64,512]{2,1,0:T(8,128)(2,1)S(1)} collective-permute-done((bf16[16,64,512]{2,1,0:T(8,128)(2,1)}, bf16[16,64,512]{2,1,0:T(8,128)(2,1)S(1)}, u32[]{:S(2)}, u32[]{:S(2)}) %collective-permute-start.10) | collective-permute-done | bytes 1048608 | tf_op jit(solution)/shard_map/ppermute | solution.py:287
  646.0 7.5 second_back.5
  659.1 14.9 %collective-permute-done.11 = bf16[16,64,512]{2,1,0:T(8,128)(2,1)S(1)} collective-permute-done((bf16[16,64,512]{2,1,0:T(8,128)(2,1)}, bf16[16,64,512]{2,1,0:T(8,128)(2,1)S(1)}, u32[]{:S(2)}, u32[]{:S(2)}) %collective-permute-start.11) | collective-permute-done | bytes 1048608 | tf_op jit(solution)/shard_map/ppermute | solution.py:287
  675.0 16.1 %all-to-all-start.10 = ((bf16[16,2,64,512]{3,2,1,0:T(8,128)(2,1)}), bf16[16,2,64,512]{3,2,1,0:T(8,128)(2,1)S(1)}, u32[]{:S(2)}, u32[]{:S(2)}) async-start(bf16[16,2,64,512]{3,2,1,0:T(8,128)(2,1)} %bitcast.58), calls=%async_computation.10 | async-start | bytes 4194304 | tf_op jit(solution)/shard_map/all_to_all | solution.py:293
  691.1 5.3 collective-permute-done.4.refs_1_.refs_3_
  701.8 13.2 %fusion.18.gate_pre = f32[32,4,16,512]{3,2,1,0:T(8,128)} fusion(f32[2048]{0:T(1024)S(1)} %copy-done.38, f32[32,4,16]{2,1,0:T(4,128)S(1)} %copy.122, bf16[2048,2048]{1,0:T(8,128)(2,1)} %all-gather.2.cloned.1.call-done, bf16[4,16,32,2048]{3,2,1,0:T(8,128)(2,1)} %param.7), kind=kOutput, calls=%fused_computation.42 | convolution fusion | flops 4311744512 | bytes 14696448 | tf_op jit(solution)/shard_map/dot_general | solution.py:18
  715.0 6.4 collective-permute-done.5
  722.4 16.5 %third.6 = (bf16[32,4,16,512]{3,2,1,0:T(8,128)(2,1)}, bf16[32,4,16,512]{3,2,1,0:T(8,128)(2,1)}, bf16[16,4,16,512]{3,2,1,0:T(8,128)(2,1)}, bf16[16,4,16,512]{3,2,1,0:T(8,128)(2,1)}, f32[4,512,32]{2,1,0:T(8,128)}) custom-call(bf16[4,512,512]{2,1,0:T(8,128)(2,1)} %select_convert_fusion.1.matrix, bf16[4,512,512]{2,1,0:T(8,128)(2,1)} %select_convert_fusion.matrix_back, ...), custom_call_target="tpu_custom_call" | custom-call | flops 3221225472 | bytes 18874368 | tf_op jit(solution)/shard_map/third/pallas_call | solution.py:258
  738.9 18.7 %collective-permute-done.12.refs_1_ = bf16[16,64,512]{2,1,0:T(8,128)(2,1)S(1)} collective-permute-done((bf16[16,64,512]{2,1,0:T(8,128)(2,1)}, bf16[16,64,512]{2,1,0:T(8,128)(2,1)S(1)}, u32[]{:S(2)}, u32[]{:S(2)}) %collective-permute-start.12) | collective-permute-done | bytes 1048608 | tf_op jit(solution)/shard_map/ppermute | solution.py:287
  758.6 7.5 second_back.6
  773.3 10.7 collective-permute-done.13
  785.1 21.5 %all-to-all-start.12 = ((bf16[16,2,64,512]{3,2,1,0:T(8,128)(2,1)}), bf16[16,2,64,512]{3,2,1,0:T(8,128)(2,1)}, u32[]{:S(2)}, u32[]{:S(2)}) async-start(bf16[16,2,64,512]{3,2,1,0:T(8,128)(2,1)} %bitcast.62), calls=%async_computation.12 | async-start | bytes 4194304 | tf_op jit(solution)/shard_map/all_to_all | solution.py:293
  812.0 13.2 %fusion.16.gate_pre = f32[32,4,16,512]{3,2,1,0:T(8,128)} fusion(f32[2048]{0:T(1024)S(1)} %copy-done.38, f32[32,4,16]{2,1,0:T(4,128)S(1)} %copy.122, bf16[2048,2048]{1,0:T(8,128)(2,1)} %all-gather.2.cloned.1.call-done, bf16[4,16,32,2048]{3,2,1,0:T(8,128)(2,1)} %param.7), kind=kOutput, calls=%fused_computation.41 | convolution fusion | flops 4311744512 | bytes 14696448 | tf_op jit(solution)/shard_map/dot_general | solution.py:18
  830.4 16.6 %third.7 = (bf16[32,4,16,512]{3,2,1,0:T(8,128)(2,1)}, bf16[32,4,16,512]{3,2,1,0:T(8,128)(2,1)}, bf16[16,4,16,512]{3,2,1,0:T(8,128)(2,1)}, bf16[16,4,16,512]{3,2,1,0:T(8,128)(2,1)}, f32[4,512,32]{2,1,0:T(8,128)}) custom-call(bf16[4,512,512]{2,1,0:T(8,128)(2,1)} %select_convert_fusion.1.matrix, bf16[4,512,512]{2,1,0:T(8,128)(2,1)} %select_convert_fusion.matrix_back, ...), custom_call_target="tpu_custom_call" | custom-call | flops 3221225472 | bytes 18874368 | tf_op jit(solution)/shard_map/third/pallas_call | solution.py:258
  847.0 16.5 %collective-permute-done.14.refs_1_ = bf16[16,64,512]{2,1,0:T(8,128)(2,1)S(1)} collective-permute-done((bf16[16,64,512]{2,1,0:T(8,128)(2,1)}, bf16[16,64,512]{2,1,0:T(8,128)(2,1)S(1)}, u32[]{:S(2)}, u32[]{:S(2)}) %collective-permute-start.14) | collective-permute-done | bytes 1048608 | tf_op jit(solution)/shard_map/ppermute | solution.py:287
  864.4 7.5 second_back.7
  875.8 11.7 collective-permute-done.15
  888.6 16.7 %all-to-all-start.14 = ((bf16[16,2,64,512]{3,2,1,0:T(8,128)(2,1)}), bf16[16,2,64,512]{3,2,1,0:T(8,128)(2,1)S(1)}, u32[]{:S(2)}, u32[]{:S(2)}) async-start(bf16[16,2,64,512]{3,2,1,0:T(8,128)(2,1)} %bitcast.66), calls=%async_computation.14 | async-start | bytes 4194304 | tf_op jit(solution)/shard_map/all_to_all | solution.py:293
  910.3 19.6 %first_back.4 = (bf16[16,2,64,512]{3,2,1,0:T(8,128)(2,1)}, f32[2,1024,64]{2,1,0:T(8,128)}) custom-call(bf16[2,1024,1024]{2,1,0:T(8,128)(2,1)} %fusion.7.matrix, bf16[16,2,64,512]{3,2,1,0:T(8,128)(2,1)} %copy-done.7, bf16[16,2,64,512]{3,2,1,0:T(8,128)(2,1)} %all-to-all-done.8.grads), custom_call_target="tpu_custom_call" | custom-call | flops 4294967296 | bytes 10485760 | tf_op jit(solution)/shard_map/first_back/pallas_call | solution.py:107
  929.9 22.7 %all-to-all-done.14.grads = bf16[16,2,64,512]{3,2,1,0:T(8,128)(2,1)S(1)} async-done(((bf16[16,2,64,512]{3,2,1,0:T(8,128)(2,1)}), bf16[16,2,64,512]{3,2,1,0:T(8,128)(2,1)S(1)}, u32[]{:S(2)}, u32[]{:S(2)}) %all-to-all-start.14) | async-done | bytes 2097184 | tf_op jit(solution)/shard_map/all_to_all | solution.py:293
  953.9 5.0 all-to-all-start.9
  958.9 19.6 %first_back.5 = (bf16[16,2,64,512]{3,2,1,0:T(8,128)(2,1)}, f32[2,1024,64]{2,1,0:T(8,128)}) custom-call(bf16[2,1024,1024]{2,1,0:T(8,128)(2,1)} %fusion.7.matrix, bf16[16,2,64,512]{3,2,1,0:T(8,128)(2,1)} %copy-done.6, bf16[16,2,64,512]{3,2,1,0:T(8,128)(2,1)} %copy-done.11), custom_call_target="tpu_custom_call" | custom-call | flops 4294967296 | bytes 10485760 | tf_op jit(solution)/shard_map/first_back/pallas_call | solution.py:107
  978.6 27.7 %all-to-all-done.9 = bf16[16,2,64,512]{3,2,1,0:T(8,128)(2,1)S(1)} async-done(((bf16[16,2,64,512]{3,2,1,0:T(8,128)(2,1)}), bf16[16,2,64,512]{3,2,1,0:T(8,128)(2,1)S(1)}, u32[]{:S(2)}, u32[]{:S(2)}) %all-to-all-start.9) | async-done | bytes 2097184 | tf_op jit(solution)/shard_map/all_to_all | solution.py:293
  1006.2 5.1 all-to-all-start.11
  1011.4 19.6 %first_back.6 = (bf16[16,2,64,512]{3,2,1,0:T(8,128)(2,1)}, f32[2,1024,64]{2,1,0:T(8,128)}) custom-call(bf16[2,1024,1024]{2,1,0:T(8,128)(2,1)} %fusion.7.matrix, bf16[16,2,64,512]{3,2,1,0:T(8,128)(2,1)} %copy-done.5, bf16[16,2,64,512]{3,2,1,0:T(8,128)(2,1)} %all-to-all-done.12.grads), custom_call_target="tpu_custom_call" | custom-call | flops 4294967296 | bytes 10485760 | tf_op jit(solution)/shard_map/first_back/pallas_call | solution.py:107
  1031.0 27.8 %all-to-all-done.11 = bf16[16,2,64,512]{3,2,1,0:T(8,128)(2,1)} async-done(((bf16[16,2,64,512]{3,2,1,0:T(8,128)(2,1)}), bf16[16,2,64,512]{3,2,1,0:T(8,128)(2,1)}, u32[]{:S(2)}, u32[]{:S(2)}) %all-to-all-start.11) | async-done | bytes 2097184 | tf_op jit(solution)/shard_map/all_to_all | solution.py:293
  1058.7 5.1 all-to-all-start.13
  1063.9 19.6 %first_back.7 = (bf16[16,2,64,512]{3,2,1,0:T(8,128)(2,1)}, f32[2,1024,64]{2,1,0:T(8,128)}) custom-call(bf16[2,1024,1024]{2,1,0:T(8,128)(2,1)} %fusion.7.matrix, bf16[16,2,64,512]{3,2,1,0:T(8,128)(2,1)} %all-to-all-done.6.values, bf16[16,2,64,512]{3,2,1,0:T(8,128)(2,1)} %copy-done.15), custom_call_target="tpu_custom_call" | custom-call | flops 4294967296 | bytes 10485760 | tf_op jit(solution)/shard_map/first_back/pallas_call | solution.py:107
  1083.5 27.7 %all-to-all-done.13 = bf16[16,2,64,512]{3,2,1,0:T(8,128)(2,1)S(1)} async-done(((bf16[16,2,64,512]{3,2,1,0:T(8,128)(2,1)}), bf16[16,2,64,512]{3,2,1,0:T(8,128)(2,1)S(1)}, u32[]{:S(2)}, u32[]{:S(2)}) %all-to-all-start.13) | async-done | bytes 2097184 | tf_op jit(solution)/shard_map/all_to_all | solution.py:293
  1111.2 5.4 all-to-all-start.15
  1123.2 7.2 maximum_bitcast_fusion
  1130.4 11.7 copy.143
  1142.1 6.0 pad_maximum_fusion
  1169.2 25.4 %convert_add_fusion = f32[2048,2048]{1,0:T(8,128)} fusion(bf16[2048,2048]{1,0:T(8,128)(2,1)} %bitcast.164, bf16[2048,2048]{1,0:T(8,128)(2,1)} %all-gather.2.cloned.1.call-done, bf16[2048,512]{1,0:T(8,128)(2,1)} %bitcast.67, bf16[2048,512]{1,0:T(8,128)(2,1)} %bitcast.170, bf16[2048,512]{1,0:T(8,128)(2,1)} %bitcast.59, bf16[2048,512]{1,0:T(8,128)(2,1)S(1)} %bitcast.169), kind=kOutput, calls=%fused_computation.9 | convolution fusion | flops 17217617920 | bytes 41943040 | tf_op jit(solution)/shard_map/tc,rc->tr/dot_general | solution.py:379
  1194.6 16.7 %fusion.5 = f32[32,4,16]{2,1,0:T(4,128)S(1)} fusion(f32[32,4,16,2048]{3,2,1,0:T(8,128)} %bitcast.160, f32[2048]{0:T(1024)S(1)} %copy-done.38, bf16[4,16,32,2048]{3,2,1,0:T(8,128)(2,1)} %param.7), kind=kLoop, calls=%fused_computation.8 | loop fusion | flops 16775168 | bytes 25182208 | tf_op jit(solution)/shard_map/reduce_sum | solution.py:383
  1211.4 19.7 %fusion.6 = bf16[4,16,32,2048]{3,1,0,2:T(8,128)(2,1)} fusion(f32[32,4,16]{2,1,0:T(4,128)S(1)} %broadcast_multiply_fusion, f32[32,4,16]{2,1,0:T(4,128)S(1)} %copy.137, f32[2048]{0:T(1024)S(1)} %copy-done.38, f32[32,4,16]{2,1,0:T(4,128)S(1)} %copy.122, f32[2048,2048]{1,0:T(8,128)S(1)} %copy-done.1, bf16[4,16,32,2048]{3,2,1,0:T(8,128)(2,1)} %param.13, ...), kind=kLoop, calls=%fused_computation.11 | loop fusion | flops 37748736 | bytes 41975808 | tf_op jit(solution)/shard_map/transpose | solution.py:387
  1231.1 11.6 copy.144
  (225 shorter events, 195.8 us)
Async XLA Ops:
  7.9 5.8 copy-start
  20.0 53.9 %all-to-all-start = ((bf16[16,2,64,512]{3,2,1,0:T(8,128)(2,1)}), bf16[16,2,64,512]{3,2,1,0:T(8,128)(2,1)S(1)}, u32[]{:S(2)}, u32[]{:S(2)}) async-start(bf16[16,2,64,512]{3,2,1,0:T(8,128)(2,1)} %bitcast.22), calls=%async_computation | async-start | bytes 4194304 | tf_op jit(solution)/shard_map/all_to_all | solution.py:293
  75.3 52.2 %all-to-all-start.2 = ((bf16[16,2,64,512]{3,2,1,0:T(8,128)(2,1)}), bf16[16,2,64,512]{3,2,1,0:T(8,128)(2,1)S(1)}, u32[]{:S(2)}, u32[]{:S(2)}) async-start(bf16[16,2,64,512]{3,2,1,0:T(8,128)(2,1)} %bitcast.29), calls=%async_computation.2 | async-start | bytes 4194304 | tf_op jit(solution)/shard_map/all_to_all | solution.py:293
  128.8 69.0 %all-to-all-start.4 = ((bf16[16,2,64,512]{3,2,1,0:T(8,128)(2,1)}), bf16[16,2,64,512]{3,2,1,0:T(8,128)(2,1)S(1)}, u32[]{:S(2)}, u32[]{:S(2)}) async-start(bf16[16,2,64,512]{3,2,1,0:T(8,128)(2,1)} %bitcast.36), calls=%async_computation.4 | async-start | bytes 4194304 | tf_op jit(solution)/shard_map/all_to_all | solution.py:293
  133.5 327.1 %all-gather.2.cloned.1.call-start = ((), (), s32[]{:S(2)}) async-start(), calls=%async_computation.16 | async-start | bytes 8650752 | tf_op jit(solution)/shard_map/all_gather | solution.py:318
  134.3 68.9 %copy-start.16 = (bf16[16,2,64,64]{3,2,1,0:T(8,128)(2,1)S(1)}, bf16[16,2,64,64]{3,2,1,0:T(8,128)(2,1)}, u32[]{:S(2)}) copy-start(bf16[16,2,64,64]{3,2,1,0:T(8,128)(2,1)} %param.10) | copy-start | bytes 786436
  197.7 10.8 copy-start.5
  197.8 75.0 %all-to-all-start.6 = ((bf16[16,2,64,512]{3,2,1,0:T(8,128)(2,1)}), bf16[16,2,64,512]{3,2,1,0:T(8,128)(2,1)}, u32[]{:S(2)}, u32[]{:S(2)}) async-start(bf16[16,2,64,512]{3,2,1,0:T(8,128)(2,1)} %bitcast.43), calls=%async_computation.6 | async-start | bytes 4194304 | tf_op jit(solution)/shard_map/all_to_all | solution.py:293
  272.7 52.3 %all-to-all-start.1 = ((bf16[16,2,64,512]{3,2,1,0:T(8,128)(2,1)}), bf16[16,2,64,512]{3,2,1,0:T(8,128)(2,1)S(1)}, u32[]{:S(2)}, u32[]{:S(2)}) async-start(bf16[16,2,64,512]{3,2,1,0:T(8,128)(2,1)} %first.4), calls=%async_computation.1 | async-start | bytes 4194304 | tf_op jit(solution)/shard_map/all_to_all | solution.py:293
  326.4 52.2 %all-to-all-start.3 = ((bf16[16,2,64,512]{3,2,1,0:T(8,128)(2,1)}), bf16[16,2,64,512]{3,2,1,0:T(8,128)(2,1)S(1)}, u32[]{:S(2)}, u32[]{:S(2)}) async-start(bf16[16,2,64,512]{3,2,1,0:T(8,128)(2,1)} %first.5), calls=%async_computation.3 | async-start | bytes 4194304 | tf_op jit(solution)/shard_map/all_to_all | solution.py:293
  379.9 68.7 %all-to-all-start.5 = ((bf16[16,2,64,512]{3,2,1,0:T(8,128)(2,1)}), bf16[16,2,64,512]{3,2,1,0:T(8,128)(2,1)S(1)}, u32[]{:S(2)}, u32[]{:S(2)}) async-start(bf16[16,2,64,512]{3,2,1,0:T(8,128)(2,1)} %first.6), calls=%async_computation.5 | async-start | bytes 4194304 | tf_op jit(solution)/shard_map/all_to_all | solution.py:293
  410.2 18.4 %copy-start.4 = (bf16[16,2,64,512]{3,2,1,0:T(8,128)(2,1)S(1)}, bf16[16,2,64,512]{3,2,1,0:T(8,128)(2,1)}, u32[]{:S(2)}) copy-start(bf16[16,2,64,512]{3,2,1,0:T(8,128)(2,1)} %copy-done.3) | copy-start | bytes 6291460
  430.1 26.1 %collective-permute-start = (bf16[16,64,512]{2,1,0:T(8,128)(2,1)}, bf16[16,64,512]{2,1,0:T(8,128)(2,1)}, u32[]{:S(2)}, u32[]{:S(2)}) collective-permute-start(bf16[16,64,512]{2,1,0:T(8,128)(2,1)} %get-tuple-element.130), channel_id=1, source_target_pairs={{0,1},{1,0},{2,3},{3,2},{4,5},{5,4},{6,7},{7,6},{8,9},{9,8},{10,11... | collective-permute-start | bytes 3145736 | tf_op jit(solution)/shard_map/ppermute | solution.py:287
  448.5 6.4 copy-start.47
  448.5 6.4 copy-start.48
  448.5 6.4 copy-start.49
  448.5 6.4 copy-start.50
  448.5 6.4 copy-start.51
  448.6 6.4 copy-start.52
  448.6 7.5 copy-start.37
  448.6 12.0 copy-start.38
  448.6 109.9 %all-to-all-start.7 = ((bf16[16,2,64,512]{3,2,1,0:T(8,128)(2,1)}), bf16[16,2,64,512]{3,2,1,0:T(8,128)(2,1)}, u32[]{:S(2)}, u32[]{:S(2)}) async-start(bf16[16,2,64,512]{3,2,1,0:T(8,128)(2,1)} %first.7), calls=%async_computation.7 | async-start | bytes 4194304 | tf_op jit(solution)/shard_map/all_to_all | solution.py:293
  460.5 24.6 %collective-permute-start.1 = (bf16[16,64,512]{2,1,0:T(8,128)(2,1)}, bf16[16,64,512]{2,1,0:T(8,128)(2,1)}, u32[]{:S(2)}, u32[]{:S(2)}) collective-permute-start(bf16[16,64,512]{2,1,0:T(8,128)(2,1)} %get-tuple-element.54), channel_id=1, source_target_pairs={{0,1},{1,0},{2,3},{3,2},{4,5},{5,4},{6,7},{7,6},{8,9},{9,8},{10,11... | collective-permute-start | bytes 3145736 | tf_op jit(solution)/shard_map/ppermute | solution.py:287
  501.9 23.8 %collective-permute-start.8 = (bf16[16,64,512]{2,1,0:T(8,128)(2,1)}, bf16[16,64,512]{2,1,0:T(8,128)(2,1)}, u32[]{:S(2)}, u32[]{:S(2)}) collective-permute-start(bf16[16,64,512]{2,1,0:T(8,128)(2,1)} %bitcast.191), channel_id=1, source_target_pairs={{0,1},{1,0},{2,3},{3,2},{4,5},{5,4},{6,7},{7,6},{8,9},{9,8},{10,11... | collective-permute-start | bytes 3145736 | tf_op jit(solution)/shard_map/ppermute | solution.py:287
  533.3 22.9 %collective-permute-start.9 = (bf16[16,64,512]{2,1,0:T(8,128)(2,1)}, bf16[16,64,512]{2,1,0:T(8,128)(2,1)}, u32[]{:S(2)}, u32[]{:S(2)}) collective-permute-start(bf16[16,64,512]{2,1,0:T(8,128)(2,1)} %get-tuple-element.68), channel_id=1, source_target_pairs={{0,1},{1,0},{2,3},{3,2},{4,5},{5,4},{6,7},{7,6},{8,9},{9,8},{10,11... | collective-permute-start | bytes 3145736 | tf_op jit(solution)/shard_map/ppermute | solution.py:287
  536.4 42.3 %collective-permute-start.2 = (bf16[16,64,512]{2,1,0:T(8,128)(2,1)}, bf16[16,64,512]{2,1,0:T(8,128)(2,1)S(1)}, u32[]{:S(2)}, u32[]{:S(2)}) collective-permute-start(bf16[16,64,512]{2,1,0:T(8,128)(2,1)} %get-tuple-element.132), channel_id=1, source_target_pairs={{0,1},{1,0},{2,3},{3,2},{4,5},{5,4},{6,7},{7,6},{8,9},{9,8},{10,11... | collective-permute-start | bytes 3145736 | tf_op jit(solution)/shard_map/ppermute | solution.py:287
  558.5 116.5 %all-to-all-start.8 = ((bf16[16,2,64,512]{3,2,1,0:T(8,128)(2,1)}), bf16[16,2,64,512]{3,2,1,0:T(8,128)(2,1)}, u32[]{:S(2)}, u32[]{:S(2)}) async-start(bf16[16,2,64,512]{3,2,1,0:T(8,128)(2,1)} %bitcast.54), calls=%async_computation.8 | async-start | bytes 4194304 | tf_op jit(solution)/shard_map/all_to_all | solution.py:293
  584.0 22.2 %collective-permute-start.3 = (bf16[16,64,512]{2,1,0:T(8,128)(2,1)}, bf16[16,64,512]{2,1,0:T(8,128)(2,1)S(1)}, u32[]{:S(2)}, u32[]{:S(2)}) collective-permute-start(bf16[16,64,512]{2,1,0:T(8,128)(2,1)} %get-tuple-element.57), channel_id=1, source_target_pairs={{0,1},{1,0},{2,3},{3,2},{4,5},{5,4},{6,7},{7,6},{8,9},{9,8},{10,11... | collective-permute-start | bytes 3145736 | tf_op jit(solution)/shard_map/ppermute | solution.py:287
  623.7 21.3 %collective-permute-start.10 = (bf16[16,64,512]{2,1,0:T(8,128)(2,1)}, bf16[16,64,512]{2,1,0:T(8,128)(2,1)S(1)}, u32[]{:S(2)}, u32[]{:S(2)}) collective-permute-start(bf16[16,64,512]{2,1,0:T(8,128)(2,1)} %bitcast.193), channel_id=1, source_target_pairs={{0,1},{1,0},{2,3},{3,2},{4,5},{5,4},{6,7},{7,6},{8,9},{9,8},{10,11... | collective-permute-start | bytes 3145736 | tf_op jit(solution)/shard_map/ppermute | solution.py:287
  653.5 4.5 copy-start.27
  653.5 20.5 %collective-permute-start.11 = (bf16[16,64,512]{2,1,0:T(8,128)(2,1)}, bf16[16,64,512]{2,1,0:T(8,128)(2,1)S(1)}, u32[]{:S(2)}, u32[]{:S(2)}) collective-permute-start(bf16[16,64,512]{2,1,0:T(8,128)(2,1)} %get-tuple-element.73), channel_id=1, source_target_pairs={{0,1},{1,0},{2,3},{3,2},{4,5},{5,4},{6,7},{7,6},{8,9},{9,8},{10,11... | collective-permute-start | bytes 3145736 | tf_op jit(solution)/shard_map/ppermute | solution.py:287
  655.0 41.4 %collective-permute-start.4 = (bf16[16,64,512]{2,1,0:T(8,128)(2,1)}, bf16[16,64,512]{2,1,0:T(8,128)(2,1)S(1)}, u32[]{:S(2)}, u32[]{:S(2)}) collective-permute-start(bf16[16,64,512]{2,1,0:T(8,128)(2,1)} %get-tuple-element.134), channel_id=1, source_target_pairs={{0,1},{1,0},{2,3},{3,2},{4,5},{5,4},{6,7},{7,6},{8,9},{9,8},{10,11... | collective-permute-start | bytes 3145736 | tf_op jit(solution)/shard_map/ppermute | solution.py:287
  675.0 110.1 %all-to-all-start.10 = ((bf16[16,2,64,512]{3,2,1,0:T(8,128)(2,1)}), bf16[16,2,64,512]{3,2,1,0:T(8,128)(2,1)S(1)}, u32[]{:S(2)}, u32[]{:S(2)}) async-start(bf16[16,2,64,512]{3,2,1,0:T(8,128)(2,1)} %bitcast.58), calls=%async_computation.10 | async-start | bytes 4194304 | tf_op jit(solution)/shard_map/all_to_all | solution.py:293
  701.8 19.6 %collective-permute-start.5 = (bf16[16,64,512]{2,1,0:T(8,128)(2,1)}, bf16[16,64,512]{2,1,0:T(8,128)(2,1)S(1)}, u32[]{:S(2)}, u32[]{:S(2)}) collective-permute-start(bf16[16,64,512]{2,1,0:T(8,128)(2,1)} %get-tuple-element.60), channel_id=1, source_target_pairs={{0,1},{1,0},{2,3},{3,2},{4,5},{5,4},{6,7},{7,6},{8,9},{9,8},{10,11... | collective-permute-start | bytes 3145736 | tf_op jit(solution)/shard_map/ppermute | solution.py:287
  738.9 18.7 %collective-permute-start.12 = (bf16[16,64,512]{2,1,0:T(8,128)(2,1)}, bf16[16,64,512]{2,1,0:T(8,128)(2,1)S(1)}, u32[]{:S(2)}, u32[]{:S(2)}) collective-permute-start(bf16[16,64,512]{2,1,0:T(8,128)(2,1)} %bitcast.194), channel_id=1, source_target_pairs={{0,1},{1,0},{2,3},{3,2},{4,5},{5,4},{6,7},{7,6},{8,9},{9,8},{10,11... | collective-permute-start | bytes 3145736 | tf_op jit(solution)/shard_map/ppermute | solution.py:287
  766.1 6.1 copy-start.26
  766.1 17.9 %collective-permute-start.13 = (bf16[16,64,512]{2,1,0:T(8,128)(2,1)}, bf16[16,64,512]{2,1,0:T(8,128)(2,1)S(1)}, u32[]{:S(2)}, u32[]{:S(2)}) collective-permute-start(bf16[16,64,512]{2,1,0:T(8,128)(2,1)} %get-tuple-element.78), channel_id=1, source_target_pairs={{0,1},{1,0},{2,3},{3,2},{4,5},{5,4},{6,7},{7,6},{8,9},{9,8},{10,11... | collective-permute-start | bytes 3145736 | tf_op jit(solution)/shard_map/ppermute | solution.py:287
  769.3 37.3 %collective-permute-start.6 = (bf16[16,64,512]{2,1,0:T(8,128)(2,1)}, bf16[16,64,512]{2,1,0:T(8,128)(2,1)S(1)}, u32[]{:S(2)}, u32[]{:S(2)}) collective-permute-start(bf16[16,64,512]{2,1,0:T(8,128)(2,1)} %get-tuple-element.136), channel_id=1, source_target_pairs={{0,1},{1,0},{2,3},{3,2},{4,5},{5,4},{6,7},{7,6},{8,9},{9,8},{10,11... | collective-permute-start | bytes 3145736 | tf_op jit(solution)/shard_map/ppermute | solution.py:287
  785.1 40.1 %copy-start.11 = (bf16[16,2,64,512]{3,2,1,0:T(8,128)(2,1)}, bf16[16,2,64,512]{3,2,1,0:T(8,128)(2,1)S(1)}, u32[]{:S(2)}) copy-start(bf16[16,2,64,512]{3,2,1,0:T(8,128)(2,1)S(1)} %all-to-all-done.10.grads) | copy-start | bytes 6291460
  785.1 103.5 %all-to-all-start.12 = ((bf16[16,2,64,512]{3,2,1,0:T(8,128)(2,1)}), bf16[16,2,64,512]{3,2,1,0:T(8,128)(2,1)}, u32[]{:S(2)}, u32[]{:S(2)}) async-start(bf16[16,2,64,512]{3,2,1,0:T(8,128)(2,1)} %bitcast.62), calls=%async_computation.12 | async-start | bytes 4194304 | tf_op jit(solution)/shard_map/all_to_all | solution.py:293
  812.0 17.3 %collective-permute-start.7 = (bf16[16,64,512]{2,1,0:T(8,128)(2,1)}, bf16[16,64,512]{2,1,0:T(8,128)(2,1)S(1)}, u32[]{:S(2)}, u32[]{:S(2)}) collective-permute-start(bf16[16,64,512]{2,1,0:T(8,128)(2,1)} %get-tuple-element.63), channel_id=1, source_target_pairs={{0,1},{1,0},{2,3},{3,2},{4,5},{5,4},{6,7},{7,6},{8,9},{9,8},{10,11... | collective-permute-start | bytes 3145736 | tf_op jit(solution)/shard_map/ppermute | solution.py:287
  846.9 16.5 %collective-permute-start.14 = (bf16[16,64,512]{2,1,0:T(8,128)(2,1)}, bf16[16,64,512]{2,1,0:T(8,128)(2,1)S(1)}, u32[]{:S(2)}, u32[]{:S(2)}) collective-permute-start(bf16[16,64,512]{2,1,0:T(8,128)(2,1)} %bitcast.192), channel_id=1, source_target_pairs={{0,1},{1,0},{2,3},{3,2},{4,5},{5,4},{6,7},{7,6},{8,9},{9,8},{10,11... | collective-permute-start | bytes 3145736 | tf_op jit(solution)/shard_map/ppermute | solution.py:287
  871.9 15.6 %collective-permute-start.15 = (bf16[16,64,512]{2,1,0:T(8,128)(2,1)}, bf16[16,64,512]{2,1,0:T(8,128)(2,1)S(1)}, u32[]{:S(2)}, u32[]{:S(2)}) collective-permute-start(bf16[16,64,512]{2,1,0:T(8,128)(2,1)} %get-tuple-element.83), channel_id=1, source_target_pairs={{0,1},{1,0},{2,3},{3,2},{4,5},{5,4},{6,7},{7,6},{8,9},{9,8},{10,11... | collective-permute-start | bytes 3145736 | tf_op jit(solution)/shard_map/ppermute | solution.py:287
  873.5 31.8 %copy-start.17 = (bf16[16,2,64,64]{3,2,1,0:T(8,128)(2,1)S(1)}, bf16[16,2,64,64]{3,2,1,0:T(8,128)(2,1)}, u32[]{:S(2)}) copy-start(bf16[16,2,64,64]{3,2,1,0:T(8,128)(2,1)} %param.10) | copy-start | bytes 786436
  875.8 29.9 %copy-start.40 = (s32[1024]{0:T(1024)S(1)}, s32[1024]{0:T(1024)}, u32[]{:S(2)}) copy-start(s32[1024]{0:T(1024)} %copy-done.39) | copy-start | bytes 12292
  875.8 29.9 %copy-start.42 = (s32[1024]{0:T(1024)S(1)}, s32[1024]{0:T(1024)}, u32[]{:S(2)}) copy-start(s32[1024]{0:T(1024)} %copy-done.41) | copy-start | bytes 12292
  875.8 29.9 %copy-start.46 = (pred[1024]{0:T(1024)(128)(4,1)S(1)}, pred[1024]{0:T(1024)(128)(4,1)}, u32[]{:S(2)}) copy-start(pred[1024]{0:T(1024)(128)(4,1)} %copy-done.45) | copy-start | bytes 3076
  888.6 64.0 %all-to-all-start.14 = ((bf16[16,2,64,512]{3,2,1,0:T(8,128)(2,1)}), bf16[16,2,64,512]{3,2,1,0:T(8,128)(2,1)S(1)}, u32[]{:S(2)}, u32[]{:S(2)}) async-start(bf16[16,2,64,512]{3,2,1,0:T(8,128)(2,1)} %bitcast.66), calls=%async_computation.14 | async-start | bytes 4194304 | tf_op jit(solution)/shard_map/all_to_all | solution.py:293
  953.9 52.4 %all-to-all-start.9 = ((bf16[16,2,64,512]{3,2,1,0:T(8,128)(2,1)}), bf16[16,2,64,512]{3,2,1,0:T(8,128)(2,1)S(1)}, u32[]{:S(2)}, u32[]{:S(2)}) async-start(bf16[16,2,64,512]{3,2,1,0:T(8,128)(2,1)} %get-tuple-element.69), calls=%async_computation.9 | async-start | bytes 4194304 | tf_op jit(solution)/shard_map/all_to_all | solution.py:293
  1006.2 24.7 %copy-start.12 = (bf16[16,2,64,512]{3,2,1,0:T(8,128)(2,1)}, bf16[16,2,64,512]{3,2,1,0:T(8,128)(2,1)S(1)}, u32[]{:S(2)}) copy-start(bf16[16,2,64,512]{3,2,1,0:T(8,128)(2,1)S(1)} %all-to-all-done.9) | copy-start | bytes 6291460
  1006.2 52.5 %all-to-all-start.11 = ((bf16[16,2,64,512]{3,2,1,0:T(8,128)(2,1)}), bf16[16,2,64,512]{3,2,1,0:T(8,128)(2,1)}, u32[]{:S(2)}, u32[]{:S(2)}) async-start(bf16[16,2,64,512]{3,2,1,0:T(8,128)(2,1)} %get-tuple-element.74), calls=%async_computation.11 | async-start | bytes 4194304 | tf_op jit(solution)/shard_map/all_to_all | solution.py:293
  1058.7 52.4 %all-to-all-start.13 = ((bf16[16,2,64,512]{3,2,1,0:T(8,128)(2,1)}), bf16[16,2,64,512]{3,2,1,0:T(8,128)(2,1)S(1)}, u32[]{:S(2)}, u32[]{:S(2)}) async-start(bf16[16,2,64,512]{3,2,1,0:T(8,128)(2,1)} %get-tuple-element.79), calls=%async_computation.13 | async-start | bytes 4194304 | tf_op jit(solution)/shard_map/all_to_all | solution.py:293
  1083.5 33.1 %copy-start.36 = (f32[4,16,32]{2,1,0:T(8,128)S(1)}, f32[4,16,32]{2,1,0:T(8,128)}, u32[]{:S(2)}) copy-start(f32[4,16,32]{2,1,0:T(8,128)} %copy-done.35) | copy-start | bytes 24580
  1111.2 5.5 copy-start.14
  1111.2 58.0 %all-to-all-start.15 = ((bf16[16,2,64,512]{3,2,1,0:T(8,128)(2,1)}), bf16[16,2,64,512]{3,2,1,0:T(8,128)(2,1)}, u32[]{:S(2)}, u32[]{:S(2)}) async-start(bf16[16,2,64,512]{3,2,1,0:T(8,128)(2,1)} %get-tuple-element.84), calls=%async_computation.15 | async-start | bytes 4194304 | tf_op jit(solution)/shard_map/all_to_all | solution.py:293
  1130.4 11.7 copy-start.18
  1130.4 11.7 copy-start.19
  1130.4 11.7 copy-start.20
  1142.1 6.0 copy-start.21
  1142.1 6.0 copy-start.22
  1142.1 6.0 copy-start.23
  1142.1 6.0 copy-start.24
  1160.6 5.1 copy-start.25
  1194.6 16.8 %copy-start.1 = (f32[2048,2048]{1,0:T(8,128)S(1)}, f32[2048,2048]{1,0:T(8,128)}, u32[]{:S(2)}) copy-start(f32[2048,2048]{1,0:T(8,128)} %convert_add_fusion) | copy-start | bytes 50331652
  (23 other events, 39.4 us)
Sparse Core Ops, SparseCore 0:
  137.5 122.2 all-gather.1

commit v2 on v1

v2 whole, which is shorter than its diff:
```python
import functools
import math

import jax
import jax.numpy as jnp
from jax import lax
from jax.experimental import pallas as pl
from jax.experimental.pallas import tpu as pltpu
from jax.sharding import PartitionSpec as P


EPSILON = 1e-06
F32 = jnp.float32
BF16 = jnp.bfloat16
CHUNKS = 4
GROUPS = (1, 1, 2)
LIMIT = 60 * 1024 * 1024


def dot(left, right):
    return jnp.dot(left, right, preferred_element_type=F32)


def dot_last(left, right):
    return lax.dot_general(left, right, (((1,), (1,)), ((), ())), preferred_element_type=F32)


def position(shape, axis, inner, extent):
    return (lax.broadcasted_iota(jnp.int32, shape, axis) // inner) % extent


def widen(rows, inner, extent, lanes):
    _, count, width = rows.shape
    wide = width * extent
    source = lax.broadcasted_iota(jnp.int32, (width, wide), 0)
    column = lax.broadcasted_iota(jnp.int32, (width, wide), 1)
    pick = (source == (column // (extent * lanes)) * lanes + column % lanes).astype(BF16)
    full = jnp.einsum("brq,qw->brw", rows, pick, preferred_element_type=F32)
    keep = position((count, wide), 0, inner, extent) == position((count, wide), 1, lanes, extent)
    return jnp.where(keep[None], full, 0.0).astype(BF16)


def fold(total, inner, extent, lanes):
    count, wide = total.shape
    width = wide // extent
    keep = position((count, wide), 0, inner, extent) == position((count, wide), 1, lanes, extent)
    source = lax.broadcasted_iota(jnp.int32, (wide, width), 1)
    column = lax.broadcasted_iota(jnp.int32, (wide, width), 0)
    pick = (source == (column // (extent * lanes)) * lanes + column % lanes).astype(F32)
    return jnp.dot(
        jnp.where(keep, total, 0.0), pick, precision=lax.Precision.HIGHEST, preferred_element_type=F32
    )


def params(count):
    return pltpu.CompilerParams(
        dimension_semantics=("arbitrary",) * count, vmem_limit_bytes=LIMIT
    )


def cost(flops, moved):
    return pl.CostEstimate(flops=int(flops), bytes_accessed=int(moved), transcendentals=0)


def put(held, start, values):
    for tile in range(held.shape[0]):
        held[tile, start : start + values.shape[0], :] = values[:, tile * 128 : (tile + 1) * 128]


def take(held, start, count, stride):
    tiles = [held[tile, pl.ds(start, count, stride=stride), :] for tile in range(held.shape[0])]
    return jnp.concatenate(tiles, axis=-1)


def held_rows(rows, channels):
    return [pltpu.VMEM((channels // 128, rows, 128), F32)]


def first_kernel(matrix, values, out):
    shape = out.shape
    flat = values[...].reshape(-1, shape[3])
    out[...] = dot(matrix[0], flat).astype(BF16).reshape(shape)


def first_level(matrix, values, offset, width):
    away, low, rows, _ = values.shape
    if rows % 16:
        values = lax.slice_in_dim(values, offset * width, (offset + 1) * width, axis=3)
        flat = values.transpose(1, 0, 2, 3).reshape(low, away * rows, width)
        mixed = jnp.einsum("krs,ksc->krc", matrix, flat, preferred_element_type=F32).astype(BF16)
        return mixed.reshape(low, away, rows, width).transpose(1, 0, 2, 3)
    size = away * rows
    tile = min(width, 256)
    start = offset * (width // tile)
    spec = pl.BlockSpec((away, 1, rows, tile), lambda k, c: (0, k, 0, c + start))
    return pl.pallas_call(
        first_kernel,
        grid=(low, width // tile),
        in_specs=[pl.BlockSpec((1, size, size), lambda k, c: (k, 0, 0)), spec],
        out_specs=pl.BlockSpec((away, 1, rows, tile), lambda k, c: (0, k, 0, c)),
        out_shape=jax.ShapeDtypeStruct((away, low, rows, width), BF16),
        compiler_params=params(2),
        cost_estimate=cost(
            2 * low * size * size * width, 4 * low * size * width + 2 * matrix.size
        ),
        name="first",
    )(matrix, values)


def first_grad_kernel(lanes, values, grads, total):
    width = values.shape[3]
    flat = values[...].reshape(-1, width)
    grad = grads[...].reshape(-1, width)
    total[0] = fold(dot_last(grad, flat), 1, lanes, 1)


def first_grad(values, offset, grads, lanes):
    away, low, rows, width = grads.shape
    size = away * rows
    if rows % 16:
        values = lax.slice_in_dim(values, offset * width, (offset + 1) * width, axis=3)
        flat = values.transpose(1, 0, 2, 3).reshape(low, size, width)
        grad = grads.transpose(1, 0, 2, 3).reshape(low, size, width)
        full = jnp.einsum("krc,ksc->krs", grad, flat, preferred_element_type=F32)
        return jnp.stack([fold(full[k], 1, lanes, 1) for k in range(low)])
    halves = 2 if away % 2 == 0 else 1
    return pl.pallas_call(
        functools.partial(first_grad_kernel, lanes),
        grid=(low, halves),
        in_specs=[
            pl.BlockSpec((away, 1, rows, width), lambda k, h: (0, k, 0, offset)),
            pl.BlockSpec((away // halves, 1, rows, width), lambda k, h: (h, k, 0, 0)),
        ],
        out_specs=pl.BlockSpec((1, size // halves, size // lanes), lambda k, h: (k, h, 0)),
        out_shape=jax.ShapeDtypeStruct((low, size, size // lanes), F32),
        compiler_params=params(2),
        cost_estimate=cost(2 * low * size * size * width, 4 * grads.size),
        name="first_grad",
    )(values, grads)


def second_kernel(parts, matrix, *refs):
    ins, outs = refs[:parts], refs[parts:]
    rows = outs[0].shape[1]
    for k in range(matrix.shape[0]):
        flat = jnp.concatenate([ref[k] for ref in ins], axis=0)
        mixed = dot(matrix[k], flat).astype(BF16)
        for part in range(parts):
            outs[part][k] = mixed[part * rows : (part + 1) * rows]


def second_level(matrix, pieces):
    parts = len(pieces)
    count, rows, width = pieces[0].shape
    if rows % 16:
        flat = jnp.concatenate(pieces, axis=1)
        mixed = jnp.einsum("krs,ksc->krc", matrix, flat, preferred_element_type=F32).astype(BF16)
        return tuple(jnp.split(mixed, parts, axis=1))
    step = 4 if count % 4 == 0 else 1
    size = parts * rows
    spec = pl.BlockSpec((step, rows, width), lambda k: (k, 0, 0))
    return pl.pallas_call(
        functools.partial(second_kernel, parts),
        grid=(count // step,),
        in_specs=[pl.BlockSpec((step, size, size), lambda k: (k, 0, 0))] + [spec] * parts,
        out_specs=(spec,) * parts,
        out_shape=(jax.ShapeDtypeStruct(pieces[0].shape, BF16),) * parts,
        compiler_params=params(1),
        cost_estimate=cost(2 * count * size * size * width, 4 * parts * pieces[0].size),
        name="second",
    )(matrix, *pieces)


def second_back_kernel(parts, inner, lanes, matrix, *refs):
    grads, values = refs[:parts], refs[parts : 2 * parts]
    outs, total = refs[2 * parts : 3 * parts], refs[3 * parts]
    rows = outs[0].shape[1]
    for k in range(matrix.shape[0]):
        grad = jnp.concatenate([ref[k] for ref in grads], axis=0)
        flat = jnp.concatenate([ref[k] for ref in values], axis=0)
        mixed = dot(matrix[k], grad).astype(BF16)
        for part in range(parts):
            outs[part][k] = mixed[part * rows : (part + 1) * rows]
        total[k] = fold(dot_last(grad, flat), inner, lanes, inner)


def second_back(matrix, grads, values, inner, lanes):
    parts = len(grads)
    count, rows, width = grads[0].shape
    size = parts * rows
    if rows % 16:
        grad = jnp.concatenate(grads, axis=1)
        flat = jnp.concatenate(values, axis=1)
        mixed = jnp.einsum("krs,ksc->krc", matrix, grad, preferred_element_type=F32).astype(BF16)
        full = jnp.einsum("krc,ksc->krs", grad, flat, preferred_element_type=F32)
        total = jnp.stack([fold(full[k], inner, lanes, inner) for k in range(count)])
        return (tuple(jnp.split(mixed, parts, axis=1)), total)
    step = 4 if count % 4 == 0 else 1
    spec = pl.BlockSpec((step, rows, width), lambda k: (k, 0, 0))
    result = pl.pallas_call(
        functools.partial(second_back_kernel, parts, inner, lanes),
        grid=(count // step,),
        in_specs=[pl.BlockSpec((step, size, size), lambda k: (k, 0, 0))] + [spec] * (2 * parts),
        out_specs=(spec,) * parts
        + (pl.BlockSpec((step, size, size // lanes), lambda k: (k, 0, 0)),),
        out_shape=(jax.ShapeDtypeStruct(grads[0].shape, BF16),) * parts
        + (jax.ShapeDtypeStruct((count, size, size // lanes), F32),),
        compiler_params=params(1),
        cost_estimate=cost(4 * count * size * size * width, 6 * parts * grads[0].size),
        name="second_back",
    )(matrix, *grads, *values)
    return (result[:parts], result[parts])


def gate_math(mixed, gate_pre, tokens, upstream):
    gate_sigmoid = jax.nn.sigmoid(gate_pre)
    gate_value = gate_pre * gate_sigmoid
    output = tokens.astype(F32) + mixed * gate_value
    upstream = upstream.astype(F32)
    grad_mixed = (upstream * gate_value).astype(BF16)
    grad_gate = (
        upstream * mixed * gate_sigmoid * (1.0 + gate_pre * (1.0 - gate_sigmoid))
    ).astype(BF16)
    return (output, grad_mixed, grad_gate)


def third_kernel(parts, lanes, kept, matrix, matrix_back, gate_pre, tokens, upstream, *refs):
    ins = refs[:parts]
    output, grad_gate = refs[parts + kept : parts + kept + 2]
    outs, total = refs[parts + kept + 2 : 2 * parts + kept + 2], refs[2 * parts + kept + 2]
    held = refs[2 * parts + kept + 3]
    shape = grad_gate.shape
    width = shape[3]
    flat = jnp.concatenate([ref[...].reshape(-1, width) for ref in ins], axis=0)
    mixed = dot(matrix[0], flat)
    result, grad_mixed, gate_grad = gate_math(
        mixed,
        gate_pre[...].reshape(-1, width),
        tokens[...].reshape(-1, width),
        upstream[...].reshape(-1, width),
    )
    put(held, 0, result)
    for lane in range(lanes):
        output[0, lane] = take(held, lane, shape[0], lanes).astype(BF16)
    grad_gate[...] = gate_grad.reshape(shape)
    back = dot(matrix_back[0], grad_mixed).astype(BF16)
    rows = back.shape[0] // parts
    for part in range(parts):
        outs[part][...] = back[part * rows : (part + 1) * rows].reshape(outs[part].shape)
    total[0] = fold(dot_last(grad_mixed, flat), 1, lanes, 1)


def third_level(matrix, matrix_back, gate_pre, tokens, upstream, offset, pieces, kept):
    parts = len(pieces)
    low, heads, lanes, width = pieces[0].shape
    count = low * parts
    size = count * lanes
    if lanes % 16:
        flat = jnp.concatenate(pieces, axis=0).transpose(1, 0, 2, 3).reshape(heads, size, width)
        mixed = jnp.einsum("irs,isc->irc", matrix, flat, preferred_element_type=F32)

        def turn_back(value):
            return value.reshape(heads, count, lanes, width).transpose(1, 0, 2, 3)

        def local(value):
            value = lax.slice_in_dim(value, offset * width, (offset + 1) * width, axis=3)
            return value.transpose(1, 0, 2, 3).reshape(heads, size, width)

        pre = gate_pre.transpose(1, 0, 2, 3).reshape(heads, size, width)
        result, grad_mixed, gate_grad = gate_math(mixed, pre, local(tokens), local(upstream))
        back = jnp.einsum("irs,isc->irc", matrix_back, grad_mixed, preferred_element_type=F32)
        full = jnp.einsum("irc,isc->irs", grad_mixed, flat, preferred_element_type=F32)
        total = jnp.stack([fold(full[i], 1, lanes, 1) for i in range(heads)])
        outs = tuple(jnp.split(turn_back(back.astype(BF16)), parts, axis=0))
        result = turn_back(result).astype(BF16).transpose(1, 2, 0, 3)
        gate_grad = turn_back(gate_grad)
        if kept:
            result = jnp.concatenate([kept[0], result], axis=3)
            gate_grad = jnp.concatenate([kept[1], gate_grad], axis=3)
        return (result, gate_grad, outs, total)
    channels = tokens.shape[3]
    whole = pl.BlockSpec((count, 1, lanes, width), lambda i: (0, i, 0, 0))
    shifted = pl.BlockSpec((count, 1, lanes, width), lambda i: (0, i, 0, offset))
    natural = pl.BlockSpec((1, lanes, count, width), lambda i: (i, 0, 0, offset))
    part = pl.BlockSpec((low, 1, lanes, width), lambda i: (0, i, 0, 0))
    square = pl.BlockSpec((1, size, size), lambda i: (i, 0, 0))
    first = 5 + parts
    result = pl.pallas_call(
        functools.partial(third_kernel, parts, lanes, len(kept)),
        grid=(heads,),
        in_specs=[square, square, whole, shifted, shifted]
        + [part] * parts
        + [pl.BlockSpec(memory_space=pl.ANY)] * len(kept),
        out_specs=(natural, shifted)
        + (part,) * parts
        + (pl.BlockSpec((1, size, count), lambda i: (i, 0, 0)),),
        out_shape=(
            jax.ShapeDtypeStruct((heads, lanes, count, channels), BF16),
            jax.ShapeDtypeStruct((count, heads, lanes, channels), BF16),
        )
        + (jax.ShapeDtypeStruct(pieces[0].shape, BF16),) * parts
        + (jax.ShapeDtypeStruct((heads, size, count), F32),),
        scratch_shapes=held_rows(size, width),
        input_output_aliases={first + n: n for n in range(len(kept))},
        compiler_params=params(1),
        cost_estimate=cost(6 * heads * size * size * width, 18 * heads * size * width),
        name="third",
    )(matrix, matrix_back, gate_pre, tokens, upstream, *pieces, *kept)
    return (result[0], result[1], result[2 : parts + 2], result[parts + 2])


def enter_math(values, gain):
    scale = lax.rsqrt(jnp.mean(values * values, axis=-1, keepdims=True) + EPSILON)
    return (values * scale * gain).astype(BF16)


def head_kernel(tokens, gain, chunk, held):
    values = tokens[0].astype(F32)
    width = chunk.shape[3]
    scale = lax.rsqrt(jnp.mean(values * values, axis=-1, keepdims=True) + EPSILON)
    result = values[..., :width] * scale * gain[:, :width].reshape(1, 1, width)
    put(held, 0, result.reshape(-1, width))
    step, lanes = chunk.shape[0], chunk.shape[2]
    for k in range(step):
        chunk[k, 0] = take(held, k, lanes, step).astype(BF16)


def enter_kernel(tokens, gain, turned, normed, *refs):
    chunks, held = refs[:-1], refs[-1]
    step, lanes = turned.shape[0], turned.shape[2]
    put(held, 0, tokens[0].astype(F32).reshape(lanes * step, -1))
    for k in range(step):
        values = take(held, k, lanes, step)
        result = enter_math(values, gain[...])
        turned[k, 0] = values.astype(BF16)
        normed[k, 0] = result
        stop = result.shape[1]
        for chunk in reversed(chunks):
            chunk[k, 0] = result[:, stop - chunk.shape[3] : stop]
            stop -= chunk.shape[3]


def turn_kernel(values, turned, held):
    step, lanes = turned.shape[0], turned.shape[2]
    put(held, 0, values[0].astype(F32).reshape(lanes * step, -1))
    for k in range(step):
        turned[k, 0] = take(held, k, lanes, step).astype(BF16)


STEP = 16


def natural_spec(lanes, channels):
    return pl.BlockSpec((1, lanes, STEP, channels), lambda i, k: (i, 0, k, 0))


def turned_spec(lanes, channels):
    return pl.BlockSpec((STEP, 1, lanes, channels), lambda i, k: (k, i, 0, 0))


def head(tokens, gain):
    heads, lanes, count, channels = tokens.shape
    width = channels // CHUNKS
    if lanes % 16 or count % STEP:
        return enter_math(tokens.transpose(2, 0, 1, 3).astype(F32), gain)[..., :width]
    return pl.pallas_call(
        head_kernel,
        grid=(heads, count // STEP),
        in_specs=[natural_spec(lanes, channels), pl.BlockSpec((1, channels), lambda i, k: (0, 0))],
        out_specs=turned_spec(lanes, width),
        out_shape=jax.ShapeDtypeStruct((count, heads, lanes, width), BF16),
        scratch_shapes=held_rows(lanes * STEP, width),
        compiler_params=params(2),
        cost_estimate=cost(4 * tokens.size, 3 * tokens.size),
        name="head",
    )(tokens, gain.reshape(1, channels))


def enter(tokens, gain):
    heads, lanes, count, channels = tokens.shape
    width = channels // CHUNKS
    if lanes % 16 or count % STEP:
        turned = tokens.transpose(2, 0, 1, 3)
        normed = enter_math(turned.astype(F32), gain)
        edges = [sum(GROUPS[: n + 1]) * width for n in range(len(GROUPS) - 1)]
        return (turned, normed) + tuple(jnp.split(normed, edges, axis=3)[1:])
    full = jax.ShapeDtypeStruct((count, heads, lanes, channels), BF16)
    widths = [group * width for group in GROUPS[1:]]
    return pl.pallas_call(
        enter_kernel,
        grid=(heads, count // STEP),
        in_specs=[natural_spec(lanes, channels), pl.BlockSpec((1, channels), lambda i, k: (0, 0))],
        out_specs=(turned_spec(lanes, channels),) * 2
        + tuple(turned_spec(lanes, part) for part in widths),
        out_shape=(full, full)
        + tuple(jax.ShapeDtypeStruct((count, heads, lanes, part), BF16) for part in widths),
        scratch_shapes=held_rows(lanes * STEP, channels),
        compiler_params=params(2),
        cost_estimate=cost(8 * tokens.size, 8 * tokens.size),
        name="enter",
    )(tokens, gain.reshape(1, channels))


def turn(values):
    heads, lanes, count, channels = values.shape
    if lanes % 16 or count % STEP:
        return values.transpose(2, 0, 1, 3)
    return pl.pallas_call(
        turn_kernel,
        grid=(heads, count // STEP),
        in_specs=[natural_spec(lanes, channels)],
        out_specs=turned_spec(lanes, channels),
        out_shape=jax.ShapeDtypeStruct((count, heads, lanes, channels), BF16),
        scratch_shapes=held_rows(lanes * STEP, channels),
        compiler_params=params(2),
        cost_estimate=cost(values.size, 4 * values.size),
        name="turn",
    )(values)


def last_math(grads, back, tokens, upstream, gain):
    tokens = tokens.astype(F32)
    scale = lax.rsqrt(jnp.mean(tokens * tokens, axis=-1, keepdims=True) + EPSILON)
    weighted = (grads.astype(F32) + back.astype(F32)) * gain
    average = jnp.mean(weighted * tokens, axis=-1, keepdims=True)
    return upstream.astype(F32) + scale * weighted - tokens * (scale**3 * average)


def last_kernel(back, tokens, upstream, gain, *refs):
    grads, out, held = refs[:-2], refs[-2], refs[-1]
    step, lanes = back.shape[0], back.shape[2]
    for k in range(step):
        grad = jnp.concatenate([ref[k, 0] for ref in grads], axis=-1)
        result = last_math(grad, back[k, 0], tokens[k, 0], upstream[k, 0], gain[...])
        put(held, k * lanes, result)
    for lane in range(lanes):
        out[0, lane] = take(held, lane, step, lanes).astype(BF16)


def last(grads, back, tokens, upstream, gain):
    count, heads, lanes, channels = tokens.shape
    if lanes % 16 or count % STEP:
        result = last_math(jnp.concatenate(grads, axis=3), back, tokens, upstream, gain)
        return result.astype(BF16).transpose(1, 2, 0, 3)
    whole = turned_spec(lanes, channels)
    return pl.pallas_call(
        last_kernel,
        grid=(heads, count // STEP),
        in_specs=[whole, whole, whole, pl.BlockSpec((1, channels), lambda i, k: (0, 0))]
        + [turned_spec(lanes, grads[0].shape[3])] * len(grads),
        out_specs=natural_spec(lanes, channels),
        out_shape=jax.ShapeDtypeStruct((heads, lanes, count, channels), BF16),
        scratch_shapes=held_rows(lanes * STEP, channels),
        compiler_params=params(2),
        cost_estimate=cost(10 * tokens.size, 12 * tokens.size),
        name="last",
    )(back, tokens, upstream, gain.reshape(1, channels), *grads)


def reorder(blocks, me, sign):
    count = len(blocks)
    result = []
    for r in range(count):
        block = blocks[0]
        for n in range(1, count):
            block = jnp.where((me + sign * r) % count == n, blocks[n], block)
        result.append(block)
    return result


def reorder_along(values, axis, me, sign):
    blocks = [lax.index_in_dim(values, n, axis, keepdims=False) for n in range(values.shape[axis])]
    return jnp.stack(reorder(blocks, me, sign), axis=axis)


def exchange(blocks):
    count = len(blocks)
    return [blocks[0]] + [
        lax.ppermute(blocks[r], "sb", [(n, (n + r) % count) for n in range(count)])
        for r in range(1, count)
    ]


def pair_kernel(flag, own, other, out):
    upper = flag[0] == 1
    out[0, 0] = jnp.where(upper, other[0], own[0])
    out[0, 1] = jnp.where(upper, own[0], other[0])


def pair(upper, own, other, place):
    lead, rest, channels = own.shape[:place], own.shape[place:-1], own.shape[-1]
    count, rows = math.prod(lead), math.prod(rest)
    if rows % 16:
        ordered = [jnp.where(upper, other, own), jnp.where(upper, own, other)]
        return jnp.stack(ordered, axis=place)
    spec = pl.BlockSpec((1, rows, channels), lambda n, flag: (n, 0, 0))
    result = pl.pallas_call(
        pair_kernel,
        grid_spec=pltpu.PrefetchScalarGridSpec(
            num_scalar_prefetch=1,
            grid=(count,),
            in_specs=[spec, spec],
            out_specs=pl.BlockSpec((1, 2, rows, channels), lambda n, flag: (n, 0, 0, 0)),
        ),
        out_shape=jax.ShapeDtypeStruct((count, 2, rows, channels), BF16),
        compiler_params=params(1),
        cost_estimate=cost(own.size, 8 * own.size),
        name="pair",
    )(
        upper.astype(jnp.int32).reshape(1),
        own.reshape(count, rows, channels),
        other.reshape(count, rows, channels),
    )
    return result.reshape(lead + (2,) + rest + (channels,))


def gather_rows(rows, away, parts, me):
    spot = lax.axis_index("sa")
    bits = away.bit_length() - 1
    if away != 1 << bits:
        return lax.all_gather(rows, ("sa", "sb"), axis=0, tiled=True)

    def double(rows, place):
        bit = 1 << (bits - 1 - place)
        other = lax.ppermute(rows, "sa", [(n, n ^ bit) for n in range(away)])
        upper = (spot // bit) % 2 == 1
        return pair(upper, rows, other, place)

    for place in range(bits):
        if place == min(2, bits - 1):
            blocks = exchange([rows] * parts)
            rows = jnp.stack(reorder(blocks, me, -1), axis=place)
        rows = double(rows, place)
    return rows


def across_first(values):
    return lax.all_to_all(values, "sa", split_axis=0, concat_axis=0, tiled=True)


def body(parts, away, tokens, norm_gain, gate_weight, level_one, level_two, level_three, upstream):
    heads, lanes, thirds, channels = tokens.shape
    firsts = level_one.shape[2]
    low = thirds // away
    near = thirds // parts
    me = lax.axis_index("sb")
    width = channels // CHUNKS
    rows = heads * lanes

    weight = gather_rows(gate_weight, away, parts, me).reshape(-1, channels)

    turned, normed, *chunks = enter(tokens, norm_gain)
    chunks = [head(tokens, norm_gain)] + chunks
    token_rows = normed.reshape(-1, channels)
    spreads = []
    for n, group in enumerate(GROUPS):
        spread = across_first(chunks[n].reshape(away, low, rows, group * width))
        spreads += [(spread, offset) for offset in range(group)]
    turned_up = turn(upstream)

    one = level_one.transpose(1, 2, 0, 3).reshape(low, firsts * lanes, firsts)
    one_back = level_one.transpose(1, 3, 0, 2).reshape(low, firsts * lanes, firsts)
    matrix_one = widen(one, 1, lanes, 1)
    matrix_one_back = widen(one_back, 1, lanes, 1)

    two = level_two.reshape(heads, near, parts, lanes, parts, lanes)
    two_front = reorder_along(reorder_along(two, 2, me, 1), 4, me, -1)
    two_back = reorder_along(reorder_along(two, 2, me, -1), 4, me, 1)
    two_front = two_front.transpose(1, 2, 0, 3, 4, 5).reshape(near, parts * rows, parts * lanes)
    two_back = two_back.transpose(1, 4, 0, 5, 2, 3).reshape(near, parts * rows, parts * lanes)
    matrix_two = widen(two_front, lanes, heads, lanes)
    matrix_two_back = widen(two_back, lanes, heads, lanes)

    three = level_three.reshape(heads, lanes, thirds, parts, near)
    three_front = reorder_along(three, 3, me, -1).reshape(level_three.shape)
    three_back = reorder_along(three, 3, me, 1).reshape(level_three.shape)
    three_front = three_front.transpose(0, 2, 1, 3).reshape(heads, thirds * lanes, thirds)
    three_back = three_back.transpose(0, 3, 1, 2).reshape(heads, thirds * lanes, thirds)
    matrix_three = widen(three_front, 1, lanes, 1)
    matrix_three_back = widen(three_back, 1, lanes, 1)

    def half(values, n):
        return lax.dynamic_slice_in_dim(values, n * near, near, axis=0)

    kept, normed_grads = (), []
    total_one = total_two = total_three = 0.0
    for n in range(CHUNKS):
        at = slice(n * width, (n + 1) * width)
        mixed = first_level(matrix_one, *spreads[n], width)
        mixed = across_first(mixed)
        mixed = mixed.reshape(thirds, rows, width)
        spread_two = [half(mixed, (me + r) % parts) for r in range(parts)]
        spread_two = exchange(spread_two)
        second = second_level(matrix_two, spread_two)
        second = exchange(list(second))
        second = [piece.reshape(near, heads, lanes, width) for piece in second]
        gate_pre = dot(token_rows, weight[:, at]).reshape(thirds, heads, lanes, width)
        output, gate_grad, grads, total = third_level(
            matrix_three, matrix_three_back, gate_pre, turned, turned_up, n, second, kept
        )
        kept = (output, gate_grad)
        total_three = total_three + total
        grads = [grad.reshape(near, rows, width) for grad in grads]
        grads = exchange(grads)
        grads, total = second_back(matrix_two_back, grads, spread_two, lanes, heads)
        total_two = total_two + total
        pieces = exchange(list(grads))
        joined = jnp.concatenate(reorder(pieces, me, -1), axis=0)
        grads = across_first(joined.reshape(away, low, rows, width))
        back = first_level(matrix_one_back, grads, 0, width)
        back = across_first(back)
        total_one = total_one + first_grad(*spreads[n], grads, lanes)
        normed_grads.append(back.reshape(thirds, heads, lanes, width))

    grad_rows = gate_grad.reshape(-1, channels)
    back_term = jnp.einsum("tc,rc->tr", grad_rows, weight, preferred_element_type=F32)
    back_term = back_term.astype(BF16)
    grad_tokens = last(normed_grads, back_term.reshape(turned.shape), turned, turned_up, norm_gain)

    scale = channels ** (-0.5)
    grad_one = total_one.reshape(low, firsts, lanes, firsts).transpose(2, 0, 1, 3) * scale
    grad_two = total_two.reshape(near, parts, heads, lanes, parts, lanes)
    grad_two = reorder_along(reorder_along(grad_two, 1, me, -1), 4, me, -1)
    grad_two = grad_two.transpose(2, 0, 1, 3, 4, 5).reshape(level_two.shape) * scale
    grad_three = total_three.reshape(heads, thirds, lanes, parts, near)
    grad_three = reorder_along(grad_three, 3, me, -1).reshape(heads, thirds, lanes, thirds)
    grad_three = grad_three.transpose(0, 2, 1, 3) * scale
    return (output, grad_tokens, grad_one, grad_two, grad_three)


def solution(mesh):
    in_specs = (
        P("sa", "sb", None, None),
        P(),
        P(("sa", "sb"), None),
        P("sb", "sa", None, None),
        P("sa", "sb", None, None),
        P("sa", "sb", None, None),
        P("sa", "sb", None, None),
    )
    out_specs = (
        P("sa", "sb", None, None),
        P("sa", "sb", None, None),
        P("sb", "sa", None, None),
        P("sa", "sb", None, None),
        P("sa", "sb", None, None),
    )
    return jax.shard_map(
        functools.partial(body, mesh.shape["sb"], mesh.shape["sa"]),
        mesh=mesh,
        in_specs=in_specs,
        out_specs=out_specs,
        check_vma=False,
    )
```

time: 1260 us -> 1240 us (0.984)
  Pallas kernels: 214 us -> 304 us
  local copies, waits for them, and re-layouts: 140 us -> 72.4 us
  other arithmetic: 89.6 us -> 33.4 us
  blocking collectives: 0 us -> 52.2 us
  starting transfers between devices: 135 us -> 106 us
  waiting for transfers between devices: 563 us -> 578 us
  between operations: 15 us -> 1.59 us
    all_to_all x16 -> x14, waiting for transfers between devices: 395 us -> 226 us  [across_first(): return lax.all_to_all(values, 'sa', split_axis=0, concat_axis=0, tiled=True)]
    ppermute x0 -> x4, waiting for transfers between devices: none -> 121 us  [double(): other = lax.ppermute(rows, 'sa', [(n, n ^ bit) for n in range(away)])]
    pallas_call x12 -> x24, Pallas kernels: 166 us -> 256 us  [the longest x4 68.8 us: third_level(): pl.pallas_call(functools.partial(third_kernel, parts, lanes, len(kept)),...]
    ppermute x16 -> x17, waiting for transfers between devices: 168 us -> 231 us  [exchange(): lax.ppermute(blocks[r], 'sb', [(n, (n + r) % count) for n in range(count)])]
    all_to_all x0 -> x1, blocking collectives: none -> 52.2 us  [across_first(): return lax.all_to_all(values, 'sa', split_axis=0, concat_axis=0, tiled=True)]
    all_to_all x16 -> x14, starting transfers between devices: 129 us -> 90.6 us  [across_first(): return lax.all_to_all(values, 'sa', split_axis=0, concat_axis=0, tiled=True)]
    transpose x7 -> x1, local copies, waits for them, and re-layouts: 36.6 us -> 2.91 us  [body(): two_back.transpose(1, 4, 0, 5, 2, 3)]
    transpose x4 -> x0, other arithmetic: 32.2 us -> none  [the longest x1 19.7 us: body(): grad_tokens = grad_tokens.transpose(1, 2, 0, 3)]
  transfers between devices with their start and end apart: 33 -> 35, of which waited for: 24 -> 23; matrix products, arithmetic and copies ran while one was open for 18% -> 14% of each run, Pallas kernels for 17% -> 22%
where the time goes in v2:
time: 1240 us; the launch traced here: 1230 us
  waiting for transfers between devices  578 us (47%)
  Pallas kernels  304 us (25%)
  starting transfers between devices  106 us (9%)
  matrix products  81 us (7%)
  local copies, waits for them, and re-layouts  72.4 us (6%)
  blocking collectives  52.2 us (4%)
  other arithmetic  33.4 us (3%)
    ppermute x17, waiting for transfers between devices, exchange(): lax.ppermute(blocks[r], 'sb', [(n, (n + r) % count) for n in range(count)])  231 us
    all_to_all x14, waiting for transfers between devices, across_first(): return lax.all_to_all(values, 'sa', split_axis=0, concat_axis=0, tiled=True)  226 us
    ppermute x4, waiting for transfers between devices, double(): other = lax.ppermute(rows, 'sa', [(n, n ^ bit) for n in range(away)])  121 us
    all_to_all x14, starting transfers between devices, across_first(): return lax.all_to_all(values, 'sa', split_axis=0, concat_axis=0, tiled=True)  90.6 us
    pallas_call x4, Pallas kernels, third_level(): pl.pallas_call(functools.partial(third_kernel, parts, lanes, len(kept)),...  68.8 us
    pallas_call x4, Pallas kernels, first_grad(): pl.pallas_call(functools.partial(first_grad_kernel, lanes), grid=(low, ha...  56.1 us
    pallas_call x8, Pallas kernels, first_level(): pl.pallas_call(first_kernel, grid=(low, width // tile), in_specs=[pl.Bloc...  54.4 us
    all_to_all x1, blocking collectives, across_first(): return lax.all_to_all(values, 'sa', split_axis=0, concat_axis=0, tiled=True)  52.2 us
  transfers between devices with their start and end apart: 35, of which 23 were waited for; matrix products, arithmetic and copies ran while one was open for 14% of the time, Pallas kernels for 22%

profile of v2, /device:TPU:11, one launch (start us, length us, event | category | flops | bytes accessed | tf_op | source)
XLA Modules:
  0.0 1228.2 jit_solution(2348597437254389621)
XLA Ops:
  0.6 16.7 %enter.1 = (bf16[32,4,16,2048]{3,2,1,0:T(8,128)(2,1)}, bf16[32,4,16,2048]{3,2,1,0:T(8,128)(2,1)}, bf16[32,4,16,512]{3,2,1,0:T(8,128)(2,1)}, bf16[32,4,16,1024]{3,2,1,0:T(8,128)(2,1)}) custom-call(bf16[4,16,32,2048]{3,2,1,0:T(8,128)(2,1)} %tokens.3, f32[1,2048]{1,0:T(1,128)} %bitcast.182), custom_call_target="tpu_custom_call" | custom-call | flops 33554432 | bytes 33554432 | tf_op jit(solution)/shard_map/enter/pallas_call | solution.py:389
  17.3 6.5 all-to-all-start.3
  23.8 8.6 head.1
  32.4 38.8 %all-to-all-done.3.values = bf16[16,2,64,512]{3,2,1,0:T(8,128)(2,1)S(1)} async-done(((bf16[16,2,64,512]{3,2,1,0:T(8,128)(2,1)}), bf16[16,2,64,512]{3,2,1,0:T(8,128)(2,1)S(1)}, u32[]{:S(2)}, u32[]{:S(2)}) %all-to-all-start.3) | async-done | bytes 2097184 | tf_op jit(solution)/shard_map/all_to_all | solution.py:538
  71.3 52.2 %all_to_all.75.values = bf16[16,2,64,512]{3,2,1,0:T(8,128)(2,1)} all-to-all(bf16[16,2,64,512]{3,2,1,0:T(8,128)(2,1)} %bitcast.149), channel_id=1, replica_groups=mesh['sa'=16,'sb'=2] {'sa'}, dimensions={0} | all-to-all | bytes 4194304 | tf_op jit(solution)/shard_map/all_to_all | solution.py:538
  123.4 5.2 all-to-all-start
  134.0 6.8 first.10
  140.8 80.2 %all-to-all-done.values = bf16[16,2,64,1024]{3,2,1,0:T(8,128)(2,1)} async-done(((bf16[16,2,64,1024]{3,2,1,0:T(8,128)(2,1)}), bf16[16,2,64,1024]{3,2,1,0:T(8,128)(2,1)}, u32[]{:S(2)}, u32[]{:S(2)}) %all-to-all-start) | async-done | bytes 4194336 | tf_op jit(solution)/shard_map/all_to_all | solution.py:538
  228.0 54.2 %collective-permute-done = bf16[64,2048]{1,0:T(8,128)(2,1)S(1)} collective-permute-done((bf16[64,2048]{1,0:T(8,128)(2,1)S(1)}, bf16[64,2048]{1,0:T(8,128)(2,1)S(1)}, u32[]{:S(2)}, u32[]{:S(2)}) %collective-permute-start) | collective-permute-done | bytes 262176 | tf_op jit(solution)/shard_map/ppermute | solution.py:525
  287.9 11.5 collective-permute-done.1.other
  303.5 6.7 first.11
  310.3 7.5 all-to-all-start.6
  317.7 8.1 collective-permute-done.2
  332.1 55.1 %collective-permute-done.3 = bf16[2,2,2,64,2048]{4,3,1,0,2:T(8,128)(2,1)} collective-permute-done((bf16[2,2,2,64,2048]{4,3,1,0,2:T(8,128)(2,1)}, bf16[2,2,2,64,2048]{4,3,1,0,2:T(8,128)(2,1)}, u32[]{:S(2)}, u32[]{:S(2)}) %collective-permute-start.3) | collective-permute-done | bytes 2097184 | tf_op jit(solution)/shard_map/ppermute | solution.py:525
  397.2 6.8 first.8
  404.1 5.1 all-to-all-start.1
  439.5 12.8 %turn.1.upstream = bf16[32,4,16,2048]{3,2,1,0:T(8,128)(2,1)} custom-call(bf16[4,16,32,2048]{3,2,1,0:T(8,128)(2,1)} %values.1), custom_call_target="tpu_custom_call" | custom-call | flops 4194304 | bytes 16777216 | tf_op jit(solution)/shard_map/turn/pallas_call | solution.py:408
  458.6 7.0 first.9
  465.6 9.0 pair.7
  480.1 6.6 all-to-all-start.2
  486.7 10.5 fusion.9.gate_pre
  497.2 7.0 collective-permute-done.12
  505.2 17.2 %third.4 = (bf16[4,16,32,2048]{3,2,1,0:T(8,128)(2,1)}, bf16[32,4,16,2048]{3,2,1,0:T(8,128)(2,1)}, bf16[16,4,16,512]{3,2,1,0:T(8,128)(2,1)}, bf16[16,4,16,512]{3,2,1,0:T(8,128)(2,1)}, f32[4,512,32]{2,1,0:T(8,128)}) custom-call(bf16[4,512,512]{2,1,0:T(8,128)(2,1)} %select_convert_fusion.1.matrix, bf16[4,512,512]{2,1,0:T(8,128)(2,1)} %select_convert_fusion.matrix_back, ...), custom_call_target="tpu_custom_call" | custom-call | flops 3221225472 | bytes 18874368 | tf_op jit(solution)/shard_map/third/pallas_call | solution.py:288
  530.1 15.8 %collective-permute-done.13.refs_1_ = bf16[16,64,512]{2,1,0:T(8,128)(2,1)} collective-permute-done((bf16[16,64,512]{2,1,0:T(8,128)(2,1)}, bf16[16,64,512]{2,1,0:T(8,128)(2,1)}, u32[]{:S(2)}, u32[]{:S(2)}) %collective-permute-start.13) | collective-permute-done | bytes 1048608 | tf_op jit(solution)/shard_map/ppermute | solution.py:479
  545.9 7.5 second_back.4
  553.6 14.7 %collective-permute-done.9.refs_1_.refs_3_ = bf16[16,64,512]{2,1,0:T(8,128)(2,1)S(1)} collective-permute-done((bf16[16,64,512]{2,1,0:T(8,128)(2,1)}, bf16[16,64,512]{2,1,0:T(8,128)(2,1)S(1)}, u32[]{:S(2)}, u32[]{:S(2)}) %collective-permute-start.9) | collective-permute-done | bytes 1048608 | tf_op jit(solution)/shard_map/ppermute | solution.py:479
  573.7 17.0 %collective-permute-done.14 = bf16[16,64,512]{2,1,0:T(8,128)(2,1)S(1)} collective-permute-done((bf16[16,64,512]{2,1,0:T(8,128)(2,1)}, bf16[16,64,512]{2,1,0:T(8,128)(2,1)S(1)}, u32[]{:S(2)}, u32[]{:S(2)}) %collective-permute-start.14) | collective-permute-done | bytes 1048608 | tf_op jit(solution)/shard_map/ppermute | solution.py:479
  593.6 10.5 all-to-all-start.7
  604.1 10.5 fusion.10.gate_pre
  615.6 17.2 %third.5 = (bf16[4,16,32,2048]{3,2,1,0:T(8,128)(2,1)}, bf16[32,4,16,2048]{3,2,1,0:T(8,128)(2,1)}, bf16[16,4,16,512]{3,2,1,0:T(8,128)(2,1)}, bf16[16,4,16,512]{3,2,1,0:T(8,128)(2,1)}, f32[4,512,32]{2,1,0:T(8,128)}) custom-call(bf16[4,512,512]{2,1,0:T(8,128)(2,1)} %select_convert_fusion.1.matrix, ...), custom_call_target="tpu_custom_call", output_to_operand_aliasing={{0}: (7, {}), {1}: (8, {})} | custom-call | flops 3221225472 | bytes 18874368 | tf_op jit(solution)/shard_map/third/pallas_call | solution.py:288
  632.9 23.7 %collective-permute-done.15.refs_1_ = bf16[16,64,512]{2,1,0:T(8,128)(2,1)S(1)} collective-permute-done((bf16[16,64,512]{2,1,0:T(8,128)(2,1)}, bf16[16,64,512]{2,1,0:T(8,128)(2,1)S(1)}, u32[]{:S(2)}, u32[]{:S(2)}) %collective-permute-start.15) | collective-permute-done | bytes 1048608 | tf_op jit(solution)/shard_map/ppermute | solution.py:479
  657.6 7.5 second_back.5
  665.3 22.8 %collective-permute-done.16 = bf16[16,64,512]{2,1,0:T(8,128)(2,1)S(1)} collective-permute-done((bf16[16,64,512]{2,1,0:T(8,128)(2,1)}, bf16[16,64,512]{2,1,0:T(8,128)(2,1)S(1)}, u32[]{:S(2)}, u32[]{:S(2)}) %collective-permute-start.16) | collective-permute-done | bytes 1048608 | tf_op jit(solution)/shard_map/ppermute | solution.py:479
  691.1 8.3 all-to-all-start.9
  704.3 6.8 first.12
  711.1 35.8 %all-to-all-done.9.values.grads = bf16[16,2,64,512]{3,2,1,0:T(8,128)(2,1)} async-done(((bf16[16,2,64,512]{3,2,1,0:T(8,128)(2,1)}), bf16[16,2,64,512]{3,2,1,0:T(8,128)(2,1)}, u32[]{:S(2)}, u32[]{:S(2)}) %all-to-all-start.9) | async-done | bytes 2097184 | tf_op jit(solution)/shard_map/all_to_all | solution.py:538
  754.9 24.1 %collective-permute-done.7.refs_1_.refs_3_ = bf16[16,64,512]{2,1,0:T(8,128)(2,1)S(1)} collective-permute-done((bf16[16,64,512]{2,1,0:T(8,128)(2,1)S(1)}, bf16[16,64,512]{2,1,0:T(8,128)(2,1)S(1)}, u32[]{:S(2)}, u32[]{:S(2)}) %collective-permute-start.7) | collective-permute-done | bytes 1048608 | tf_op jit(solution)/shard_map/ppermute | solution.py:479
  784.5 6.7 first.13
  791.3 8.3 all-to-all-done.8
  804.0 10.5 fusion.11.gate_pre
  815.5 17.2 %third.6 = (bf16[4,16,32,2048]{3,2,1,0:T(8,128)(2,1)}, bf16[32,4,16,2048]{3,2,1,0:T(8,128)(2,1)}, bf16[16,4,16,512]{3,2,1,0:T(8,128)(2,1)}, bf16[16,4,16,512]{3,2,1,0:T(8,128)(2,1)}, f32[4,512,32]{2,1,0:T(8,128)}) custom-call(bf16[4,512,512]{2,1,0:T(8,128)(2,1)} %select_convert_fusion.1.matrix, ...), custom_call_target="tpu_custom_call", output_to_operand_aliasing={{0}: (7, {}), {1}: (8, {})} | custom-call | flops 3221225472 | bytes 18874368 | tf_op jit(solution)/shard_map/third/pallas_call | solution.py:288
  836.9 20.3 %collective-permute-done.17.refs_1_ = bf16[16,64,512]{2,1,0:T(8,128)(2,1)S(1)} collective-permute-done((bf16[16,64,512]{2,1,0:T(8,128)(2,1)}, bf16[16,64,512]{2,1,0:T(8,128)(2,1)S(1)}, u32[]{:S(2)}, u32[]{:S(2)}) %collective-permute-start.17) | collective-permute-done | bytes 1048608 | tf_op jit(solution)/shard_map/ppermute | solution.py:479
  858.2 7.5 second_back.6
  866.0 13.7 %collective-permute-done.5.refs_1_.refs_3_ = bf16[16,64,512]{2,1,0:T(8,128)(2,1)S(1)} collective-permute-done((bf16[16,64,512]{2,1,0:T(8,128)(2,1)S(1)}, bf16[16,64,512]{2,1,0:T(8,128)(2,1)S(1)}, u32[]{:S(2)}, u32[]{:S(2)}) %collective-permute-start.5) | collective-permute-done | bytes 1048608 | tf_op jit(solution)/shard_map/ppermute | solution.py:479
  885.2 16.9 %collective-permute-done.18 = bf16[16,64,512]{2,1,0:T(8,128)(2,1)S(1)} collective-permute-done((bf16[16,64,512]{2,1,0:T(8,128)(2,1)}, bf16[16,64,512]{2,1,0:T(8,128)(2,1)S(1)}, u32[]{:S(2)}, u32[]{:S(2)}) %collective-permute-start.18) | collective-permute-done | bytes 1048608 | tf_op jit(solution)/shard_map/ppermute | solution.py:479
  905.1 8.2 all-to-all-start.11
  913.3 10.5 fusion.12.gate_pre
  925.6 17.2 %third.7 = (bf16[4,16,32,2048]{3,2,1,0:T(8,128)(2,1)}, bf16[32,4,16,2048]{3,2,1,0:T(8,128)(2,1)}, bf16[16,4,16,512]{3,2,1,0:T(8,128)(2,1)}, bf16[16,4,16,512]{3,2,1,0:T(8,128)(2,1)}, f32[4,512,32]{2,1,0:T(8,128)}) custom-call(bf16[4,512,512]{2,1,0:T(8,128)(2,1)} %select_convert_fusion.1.matrix, ...), custom_call_target="tpu_custom_call", output_to_operand_aliasing={{0}: (7, {}), {1}: (8, {})} | custom-call | flops 3221225472 | bytes 18874368 | tf_op jit(solution)/shard_map/third/pallas_call | solution.py:288
  943.1 23.4 %collective-permute-done.19.refs_1_ = bf16[16,64,512]{2,1,0:T(8,128)(2,1)S(1)} collective-permute-done((bf16[16,64,512]{2,1,0:T(8,128)(2,1)}, bf16[16,64,512]{2,1,0:T(8,128)(2,1)S(1)}, u32[]{:S(2)}, u32[]{:S(2)}) %collective-permute-start.19) | collective-permute-done | bytes 1048608 | tf_op jit(solution)/shard_map/ppermute | solution.py:479
  967.5 7.5 second_back.7
  975.2 22.6 %collective-permute-done.20 = bf16[16,64,512]{2,1,0:T(8,128)(2,1)S(1)} collective-permute-done((bf16[16,64,512]{2,1,0:T(8,128)(2,1)}, bf16[16,64,512]{2,1,0:T(8,128)(2,1)S(1)}, u32[]{:S(2)}, u32[]{:S(2)}) %collective-permute-start.20) | collective-permute-done | bytes 1048608 | tf_op jit(solution)/shard_map/ppermute | solution.py:479
  1000.7 8.6 all-to-all-start.13
  1009.4 6.8 first.14
  1016.2 40.7 %all-to-all-done.13.values.grads = bf16[16,2,64,512]{3,2,1,0:T(8,128)(2,1)} async-done(((bf16[16,2,64,512]{3,2,1,0:T(8,128)(2,1)}), bf16[16,2,64,512]{3,2,1,0:T(8,128)(2,1)}, u32[]{:S(2)}, u32[]{:S(2)}) %all-to-all-start.13) | async-done | bytes 2097184 | tf_op jit(solution)/shard_map/all_to_all | solution.py:538
  1066.5 5.4 fusion.54
  1080.1 6.7 first.15
  1086.8 22.3 %all-to-all-done.12 = bf16[16,2,64,512]{3,2,1,0:T(8,128)(2,1)S(1)} async-done(((bf16[16,2,64,512]{3,2,1,0:T(8,128)(2,1)}), bf16[16,2,64,512]{3,2,1,0:T(8,128)(2,1)S(1)}, u32[]{:S(2)}, u32[]{:S(2)}) %all-to-all-start.12) | async-done | bytes 2097184 | tf_op jit(solution)/shard_map/all_to_all | solution.py:538
  1109.1 5.1 all-to-all-start.14
  1114.2 23.9 %convolution_convert_fusion = bf16[2048,2048]{1,0:T(8,128)(2,1)} fusion(bf16[2048,2048]{1,0:T(8,128)(2,1)} %bitcast.137, bf16[2048,2048]{1,0:T(8,128)(2,1)} %bitcast.144), kind=kOutput, calls=%fused_computation.4 | convolution fusion | flops 17184063488 | bytes 25165824 | tf_op jit(solution)/shard_map/tc,rc->tr/dot_general | solution.py:616
  1147.8 13.9 %first_grad.4 = f32[2,1024,64]{2,1,0:T(8,128)} custom-call(bf16[16,2,64,512]{3,2,1,0:T(8,128)(2,1)} %all_to_all.75.values, bf16[16,2,64,512]{3,2,1,0:T(8,128)(2,1)} %copy-done.3), custom_call_target="tpu_custom_call" | custom-call | flops 2147483648 | bytes 4194304 | tf_op jit(solution)/shard_map/first_grad/pallas_call | solution.py:127
  1161.8 14.1 %first_grad.5 = f32[2,1024,64]{2,1,0:T(8,128)} custom-call(bf16[16,2,64,512]{3,2,1,0:T(8,128)(2,1)} %copy-done.2, bf16[16,2,64,512]{3,2,1,0:T(8,128)(2,1)} %all-to-all-done.9.values.grads), custom_call_target="tpu_custom_call" | custom-call | flops 2147483648 | bytes 4194304 | tf_op jit(solution)/shard_map/first_grad/pallas_call | solution.py:127
  1175.9 13.9 %first_grad.7 = f32[2,1024,64]{2,1,0:T(8,128)} custom-call(bf16[16,2,64,1024]{3,2,1,0:T(8,128)(2,1)} %all-to-all-done.values, bf16[16,2,64,512]{3,2,1,0:T(8,128)(2,1)} %all-to-all-done.13.values.grads), custom_call_target="tpu_custom_call" | custom-call | flops 2147483648 | bytes 4194304 | tf_op jit(solution)/shard_map/first_grad/pallas_call | solution.py:127
  1189.8 14.1 %first_grad.6 = f32[2,1024,64]{2,1,0:T(8,128)} custom-call(bf16[16,2,64,1024]{3,2,1,0:T(8,128)(2,1)} %all-to-all-done.values, bf16[16,2,64,512]{3,2,1,0:T(8,128)(2,1)} %copy-done.4), custom_call_target="tpu_custom_call" | custom-call | flops 2147483648 | bytes 4194304 | tf_op jit(solution)/shard_map/first_grad/pallas_call | solution.py:127
  1206.6 21.4 %last.1 = bf16[4,16,32,2048]{3,2,1,0:T(8,128)(2,1)} custom-call(bf16[32,4,16,2048]{3,2,1,0:T(8,128)(2,1)} %bitcast.151, bf16[32,4,16,2048]{3,2,1,0:T(8,128)(2,1)} %get-tuple-element.50.tokens, bf16[32,4,16,2048]{3,2,1,0:T(8,128)(2,1)} %turn.1.upstream, f32[1,2048]{1,0:T(1,128)} %bitcast.184, bf16[32,4,16,512]{3,2,1,0:T(8,128)(2,1)} %bitcast.145, ...), custom_call_target="tpu_custom_call" | custom-call | flops 41943040 | bytes 50331648 | tf_op jit(solution)/shard_map/last/pallas_call | solution.py:446
  (219 shorter events, 177.2 us)
Async XLA Ops:
  17.3 53.9 %all-to-all-start.3 = ((bf16[16,2,64,512]{3,2,1,0:T(8,128)(2,1)}), bf16[16,2,64,512]{3,2,1,0:T(8,128)(2,1)S(1)}, u32[]{:S(2)}, u32[]{:S(2)}) async-start(bf16[16,2,64,512]{3,2,1,0:T(8,128)(2,1)} %bitcast.159), calls=%async_computation.3 | async-start | bytes 4194304 | tf_op jit(solution)/shard_map/all_to_all | solution.py:538
  71.3 52.2 %copy-start.2 = (bf16[16,2,64,512]{3,2,1,0:T(8,128)(2,1)}, bf16[16,2,64,512]{3,2,1,0:T(8,128)(2,1)S(1)}, u32[]{:S(2)}) copy-start(bf16[16,2,64,512]{3,2,1,0:T(8,128)(2,1)S(1)} %all-to-all-done.3.values) | copy-start | bytes 6291460
  123.4 97.6 %all-to-all-start = ((bf16[16,2,64,1024]{3,2,1,0:T(8,128)(2,1)}), bf16[16,2,64,1024]{3,2,1,0:T(8,128)(2,1)}, u32[]{:S(2)}, u32[]{:S(2)}) async-start(bf16[16,2,64,1024]{3,2,1,0:T(8,128)(2,1)} %bitcast.153), calls=%async_computation | async-start | bytes 8388608 | tf_op jit(solution)/shard_map/all_to_all | solution.py:538
  134.0 91.8 %copy-start.30 = (bf16[64,2048]{1,0:T(8,128)(2,1)S(1)}, bf16[64,2048]{1,0:T(8,128)(2,1)}, u32[]{:S(2)}) copy-start(bf16[64,2048]{1,0:T(8,128)(2,1)} %param.9) | copy-start | bytes 786436
  221.0 89.2 %all-to-all-start.4 = ((bf16[16,2,64,512]{3,2,1,0:T(8,128)(2,1)}), bf16[16,2,64,512]{3,2,1,0:T(8,128)(2,1)S(1)}, u32[]{:S(2)}, u32[]{:S(2)}) async-start(bf16[16,2,64,512]{3,2,1,0:T(8,128)(2,1)} %first.10), calls=%async_computation.4 | async-start | bytes 4194304 | tf_op jit(solution)/shard_map/all_to_all | solution.py:538
  225.8 56.4 %collective-permute-start = (bf16[64,2048]{1,0:T(8,128)(2,1)S(1)}, bf16[64,2048]{1,0:T(8,128)(2,1)S(1)}, u32[]{:S(2)}, u32[]{:S(2)}) collective-permute-start(bf16[64,2048]{1,0:T(8,128)(2,1)S(1)} %copy-done.30), channel_id=1, source_target_pairs={{0,16},{2,18},{4,20},{6,22},{8,24},{10,26},{12,28},{14,30},{16,0},... | collective-permute-start | bytes 786440 | tf_op jit(solution)/shard_map/ppermute | solution.py:525
  284.7 14.7 %collective-permute-start.1 = (bf16[2,64,2048]{2,1,0:T(8,128)(2,1)}, bf16[2,64,2048]{2,1,0:T(8,128)(2,1)S(1)}, u32[]{:S(2)}, u32[]{:S(2)}) collective-permute-start(bf16[2,64,2048]{2,1,0:T(8,128)(2,1)} %bitcast.157), channel_id=1, source_target_pairs={{0,8},{2,10},{4,12},{6,14},{8,0},{10,2},{12,4},{14,6},{16,24},{18,... | collective-permute-start | bytes 1572872 | tf_op jit(solution)/shard_map/ppermute | solution.py:525
  302.3 23.5 %collective-permute-start.2 = (bf16[2,2,64,2048]{3,2,1,0:T(8,128)(2,1)}, bf16[2,2,64,2048]{3,2,1,0:T(8,128)(2,1)}, u32[]{:S(2)}, u32[]{:S(2)}) collective-permute-start(bf16[2,2,64,2048]{3,2,1,0:T(8,128)(2,1)} %pair.5), channel_id=1, source_target_pairs={{0,1},{1,0},{2,3},{3,2},{4,5},{5,4},{6,7},{7,6},{8,9},{9,8},{10,11... | collective-permute-start | bytes 3145736 | tf_op jit(solution)/shard_map/ppermute | solution.py:479
  310.3 15.5 %copy-start.5 = (bf16[2,2,64,2048]{3,2,1,0:T(8,128)(2,1)S(1)}, bf16[2,2,64,2048]{3,2,1,0:T(8,128)(2,1)}, u32[]{:S(2)}) copy-start(bf16[2,2,64,2048]{3,2,1,0:T(8,128)(2,1)} %pair.5) | copy-start | bytes 3145732
  310.3 93.8 %all-to-all-start.6 = ((bf16[16,2,64,512]{3,2,1,0:T(8,128)(2,1)}), bf16[16,2,64,512]{3,2,1,0:T(8,128)(2,1)}, u32[]{:S(2)}, u32[]{:S(2)}) async-start(bf16[16,2,64,512]{3,2,1,0:T(8,128)(2,1)} %first.11), calls=%async_computation.6 | async-start | bytes 4194304 | tf_op jit(solution)/shard_map/all_to_all | solution.py:538
  328.7 58.5 %collective-permute-start.3 = (bf16[2,2,2,64,2048]{4,3,1,0,2:T(8,128)(2,1)}, bf16[2,2,2,64,2048]{4,3,1,0,2:T(8,128)(2,1)}, u32[]{:S(2)}, u32[]{:S(2)}) collective-permute-start(bf16[2,2,2,64,2048]{4,3,1,0,2:T(8,128)(2,1)} %pad_maximum_fusion), channel_id=1, source_target_pairs={{0,4},{2,6},{4,0},{6,2},{8,12},{10,14},{12,8},{14,10},{16,20},{18,... | collective-permute-start | bytes 6291464 | tf_op jit(solution)/shard_map/ppermute | solution.py:525
  395.1 70.5 %collective-permute-start.4 = (bf16[2,2,2,2,64,2048]{5,4,3,2,1,0:T(8,128)(2,1)}, bf16[2,2,2,2,64,2048]{5,4,3,2,1,0:T(8,128)(2,1)}, u32[]{:S(2)}, u32[]{:S(2)}) collective-permute-start(bf16[2,2,2,2,64,2048]{5,4,3,2,1,0:T(8,128)(2,1)} %bitcast.138), channel_id=1, source_target_pairs={{0,2},{2,0},{4,6},{6,4},{8,10},{10,8},{12,14},{14,12},{16,18},{18,... | collective-permute-start | bytes 12582920 | tf_op jit(solution)/shard_map/ppermute | solution.py:525
  404.1 76.1 %all-to-all-start.1 = ((bf16[16,2,64,512]{3,2,1,0:T(8,128)(2,1)}), bf16[16,2,64,512]{3,2,1,0:T(8,128)(2,1)}, u32[]{:S(2)}, u32[]{:S(2)}) async-start(bf16[16,2,64,512]{3,2,1,0:T(8,128)(2,1)} %first.8), calls=%async_computation.1 | async-start | bytes 4194304 | tf_op jit(solution)/shard_map/all_to_all | solution.py:538
  430.9 43.7 %collective-permute-start.11 = (bf16[16,64,512]{2,1,0:T(8,128)(2,1)}, bf16[16,64,512]{2,1,0:T(8,128)(2,1)S(1)}, u32[]{:S(2)}, u32[]{:S(2)}) collective-permute-start(bf16[16,64,512]{2,1,0:T(8,128)(2,1)} %get-tuple-element.122), channel_id=1, source_target_pairs={{0,1},{1,0},{2,3},{3,2},{4,5},{5,4},{6,7},{7,6},{8,9},{9,8},{10,11... | collective-permute-start | bytes 3145736 | tf_op jit(solution)/shard_map/ppermute | solution.py:479
  439.4 12.9 %copy-start.40 = (s32[128]{0:T(128)S(1)}, s32[128]{0:T(128)}, u32[]{:S(2)}) copy-start(s32[128]{0:T(128)} %get-tuple-element.158) | copy-start | bytes 1540
  439.4 12.9 %copy-start.42 = (s32[128]{0:T(128)S(1)}, s32[128]{0:T(128)}, u32[]{:S(2)}) copy-start(s32[128]{0:T(128)} %get-tuple-element.159) | copy-start | bytes 1540
  439.4 12.9 %copy-start.44 = (s32[128]{0:T(128)S(1)}, s32[128]{0:T(128)}, u32[]{:S(2)}) copy-start(s32[128]{0:T(128)} %get-tuple-element.160) | copy-start | bytes 1540
  439.5 12.9 %copy-start.46 = (s32[128]{0:T(128)S(1)}, s32[128]{0:T(128)}, u32[]{:S(2)}) copy-start(s32[128]{0:T(128)} %get-tuple-element.161) | copy-start | bytes 1540
  439.5 12.9 %copy-start.48 = (pred[128]{0:T(512)(128)(4,1)S(1)}, pred[128]{0:T(512)(128)(4,1)}, u32[]{:S(2)}) copy-start(pred[128]{0:T(512)(128)(4,1)} %get-tuple-element.150) | copy-start | bytes 388
  439.5 12.9 %copy-start.50 = (pred[128]{0:T(512)(128)(4,1)S(1)}, pred[128]{0:T(512)(128)(4,1)}, u32[]{:S(2)}) copy-start(pred[128]{0:T(512)(128)(4,1)} %get-tuple-element.151) | copy-start | bytes 388
  439.5 14.0 %copy-start.36 = (s32[512]{0:T(512)S(1)}, s32[512]{0:T(512)}, u32[]{:S(2)}) copy-start(s32[512]{0:T(512)} %get-tuple-element.152) | copy-start | bytes 6148
  439.5 14.0 %copy-start.37 = (s32[512]{0:T(512)S(1)}, s32[512]{0:T(512)}, u32[]{:S(2)}) copy-start(s32[512]{0:T(512)} %get-tuple-element.153) | copy-start | bytes 6148
  439.5 14.0 %copy-start.52 = (pred[512]{0:T(512)(128)(4,1)S(1)}, pred[512]{0:T(512)(128)(4,1)}, u32[]{:S(2)}) copy-start(pred[512]{0:T(512)(128)(4,1)} %fusion.51) | copy-start | bytes 1540
  439.5 17.0 %copy-start.29 = (bf16[4,16,32,32]{2,1,3,0:T(8,128)(2,1)S(1)}, bf16[4,16,32,32]{2,1,3,0:T(8,128)(2,1)}, u32[]{:S(2)}) copy-start(bf16[4,16,32,32]{2,1,3,0:T(8,128)(2,1)} %copy.76) | copy-start | bytes 393220
  479.9 24.3 %collective-permute-start.12 = (bf16[16,64,512]{2,1,0:T(8,128)(2,1)}, bf16[16,64,512]{2,1,0:T(8,128)(2,1)S(1)}, u32[]{:S(2)}, u32[]{:S(2)}) collective-permute-start(bf16[16,64,512]{2,1,0:T(8,128)(2,1)} %get-tuple-element.60), channel_id=1, source_target_pairs={{0,1},{1,0},{2,3},{3,2},{4,5},{5,4},{6,7},{7,6},{8,9},{9,8},{10,11... | collective-permute-start | bytes 3145736 | tf_op jit(solution)/shard_map/ppermute | solution.py:479
  480.1 113.4 %all-to-all-start.2 = ((bf16[16,2,64,512]{3,2,1,0:T(8,128)(2,1)}), bf16[16,2,64,512]{3,2,1,0:T(8,128)(2,1)}, u32[]{:S(2)}, u32[]{:S(2)}) async-start(bf16[16,2,64,512]{3,2,1,0:T(8,128)(2,1)} %first.9), calls=%async_computation.2 | async-start | bytes 4194304 | tf_op jit(solution)/shard_map/all_to_all | solution.py:538
  505.1 21.1 %copy-start.41 = (s32[128]{0:T(128)S(1)}, s32[128]{0:T(128)}, u32[]{:S(2)}) copy-start(s32[128]{0:T(128)} %get-tuple-element.158) | copy-start | bytes 1540
  505.1 21.1 %copy-start.43 = (s32[128]{0:T(128)S(1)}, s32[128]{0:T(128)}, u32[]{:S(2)}) copy-start(s32[128]{0:T(128)} %get-tuple-element.159) | copy-start | bytes 1540
  505.1 21.1 %copy-start.45 = (s32[128]{0:T(128)S(1)}, s32[128]{0:T(128)}, u32[]{:S(2)}) copy-start(s32[128]{0:T(128)} %get-tuple-element.160) | copy-start | bytes 1540
  505.1 21.1 %copy-start.47 = (s32[128]{0:T(128)S(1)}, s32[128]{0:T(128)}, u32[]{:S(2)}) copy-start(s32[128]{0:T(128)} %get-tuple-element.161) | copy-start | bytes 1540
  505.1 21.1 %copy-start.49 = (pred[128]{0:T(512)(128)(4,1)S(1)}, pred[128]{0:T(512)(128)(4,1)}, u32[]{:S(2)}) copy-start(pred[128]{0:T(512)(128)(4,1)} %get-tuple-element.150) | copy-start | bytes 388
  505.1 21.1 %copy-start.51 = (pred[128]{0:T(512)(128)(4,1)S(1)}, pred[128]{0:T(512)(128)(4,1)}, u32[]{:S(2)}) copy-start(pred[128]{0:T(512)(128)(4,1)} %get-tuple-element.151) | copy-start | bytes 388
  522.4 23.5 %collective-permute-start.13 = (bf16[16,64,512]{2,1,0:T(8,128)(2,1)}, bf16[16,64,512]{2,1,0:T(8,128)(2,1)}, u32[]{:S(2)}, u32[]{:S(2)}) collective-permute-start(bf16[16,64,512]{2,1,0:T(8,128)(2,1)} %bitcast.185), channel_id=1, source_target_pairs={{0,1},{1,0},{2,3},{3,2},{4,5},{5,4},{6,7},{7,6},{8,9},{9,8},{10,11... | collective-permute-start | bytes 3145736 | tf_op jit(solution)/shard_map/ppermute | solution.py:479
  528.9 39.4 %collective-permute-start.9 = (bf16[16,64,512]{2,1,0:T(8,128)(2,1)}, bf16[16,64,512]{2,1,0:T(8,128)(2,1)S(1)}, u32[]{:S(2)}, u32[]{:S(2)}) collective-permute-start(bf16[16,64,512]{2,1,0:T(8,128)(2,1)} %get-tuple-element.124), channel_id=1, source_target_pairs={{0,1},{1,0},{2,3},{3,2},{4,5},{5,4},{6,7},{7,6},{8,9},{9,8},{10,11... | collective-permute-start | bytes 3145736 | tf_op jit(solution)/shard_map/ppermute | solution.py:479
  553.3 37.4 %collective-permute-start.14 = (bf16[16,64,512]{2,1,0:T(8,128)(2,1)}, bf16[16,64,512]{2,1,0:T(8,128)(2,1)S(1)}, u32[]{:S(2)}, u32[]{:S(2)}) collective-permute-start(bf16[16,64,512]{2,1,0:T(8,128)(2,1)} %get-tuple-element.71), channel_id=1, source_target_pairs={{0,1},{1,0},{2,3},{3,2},{4,5},{5,4},{6,7},{7,6},{8,9},{9,8},{10,11... | collective-permute-start | bytes 3145736 | tf_op jit(solution)/shard_map/ppermute | solution.py:479
  573.5 41.0 %collective-permute-start.10 = (bf16[16,64,512]{2,1,0:T(8,128)(2,1)}, bf16[16,64,512]{2,1,0:T(8,128)(2,1)S(1)}, u32[]{:S(2)}, u32[]{:S(2)}) collective-permute-start(bf16[16,64,512]{2,1,0:T(8,128)(2,1)} %get-tuple-element.58), channel_id=1, source_target_pairs={{0,1},{1,0},{2,3},{3,2},{4,5},{5,4},{6,7},{7,6},{8,9},{9,8},{10,11... | collective-permute-start | bytes 3145736 | tf_op jit(solution)/shard_map/ppermute | solution.py:479
  593.6 97.5 %all-to-all-start.7 = ((bf16[16,2,64,512]{3,2,1,0:T(8,128)(2,1)}), bf16[16,2,64,512]{3,2,1,0:T(8,128)(2,1)S(1)}, u32[]{:S(2)}, u32[]{:S(2)}) async-start(bf16[16,2,64,512]{3,2,1,0:T(8,128)(2,1)} %bitcast.61), calls=%async_computation.7 | async-start | bytes 4194304 | tf_op jit(solution)/shard_map/all_to_all | solution.py:538
  632.7 23.9 %collective-permute-start.15 = (bf16[16,64,512]{2,1,0:T(8,128)(2,1)}, bf16[16,64,512]{2,1,0:T(8,128)(2,1)S(1)}, u32[]{:S(2)}, u32[]{:S(2)}) collective-permute-start(bf16[16,64,512]{2,1,0:T(8,128)(2,1)} %bitcast.188), channel_id=1, source_target_pairs={{0,1},{1,0},{2,3},{3,2},{4,5},{5,4},{6,7},{7,6},{8,9},{9,8},{10,11... | collective-permute-start | bytes 3145736 | tf_op jit(solution)/shard_map/ppermute | solution.py:479
  665.1 23.0 %collective-permute-start.16 = (bf16[16,64,512]{2,1,0:T(8,128)(2,1)}, bf16[16,64,512]{2,1,0:T(8,128)(2,1)S(1)}, u32[]{:S(2)}, u32[]{:S(2)}) collective-permute-start(bf16[16,64,512]{2,1,0:T(8,128)(2,1)} %get-tuple-element.75), channel_id=1, source_target_pairs={{0,1},{1,0},{2,3},{3,2},{4,5},{5,4},{6,7},{7,6},{8,9},{9,8},{10,11... | collective-permute-start | bytes 3145736 | tf_op jit(solution)/shard_map/ppermute | solution.py:479
  691.1 13.2 %copy-start.3 = (bf16[16,2,64,512]{3,2,1,0:T(8,128)(2,1)}, bf16[16,2,64,512]{3,2,1,0:T(8,128)(2,1)S(1)}, u32[]{:S(2)}) copy-start(bf16[16,2,64,512]{3,2,1,0:T(8,128)(2,1)S(1)} %all-to-all-done.7.values.grads) | copy-start | bytes 6291460
  691.1 55.8 %all-to-all-start.9 = ((bf16[16,2,64,512]{3,2,1,0:T(8,128)(2,1)}), bf16[16,2,64,512]{3,2,1,0:T(8,128)(2,1)}, u32[]{:S(2)}, u32[]{:S(2)}) async-start(bf16[16,2,64,512]{3,2,1,0:T(8,128)(2,1)} %bitcast.65), calls=%async_computation.9 | async-start | bytes 4194304 | tf_op jit(solution)/shard_map/all_to_all | solution.py:538
  746.9 52.7 %all-to-all-start.8 = ((bf16[16,2,64,512]{3,2,1,0:T(8,128)(2,1)}), bf16[16,2,64,512]{3,2,1,0:T(8,128)(2,1)S(1)}, u32[]{:S(2)}, u32[]{:S(2)}) async-start(bf16[16,2,64,512]{3,2,1,0:T(8,128)(2,1)} %first.12), calls=%async_computation.8 | async-start | bytes 4194304 | tf_op jit(solution)/shard_map/all_to_all | solution.py:538
  754.7 24.3 %collective-permute-start.7 = (bf16[16,64,512]{2,1,0:T(8,128)(2,1)S(1)}, bf16[16,64,512]{2,1,0:T(8,128)(2,1)S(1)}, u32[]{:S(2)}, u32[]{:S(2)}) collective-permute-start(bf16[16,64,512]{2,1,0:T(8,128)(2,1)S(1)} %get-tuple-element.126), channel_id=1, source_target_pairs={{0,1},{1,0},{2,3},{3,2},{4,5},{5,4},{6,7},{7,6},{8,9},{9,8},{10,11... | collective-permute-start | bytes 3145736 | tf_op jit(solution)/shard_map/ppermute | solution.py:479
  784.3 30.2 %collective-permute-start.8 = (bf16[16,64,512]{2,1,0:T(8,128)(2,1)}, bf16[16,64,512]{2,1,0:T(8,128)(2,1)S(1)}, u32[]{:S(2)}, u32[]{:S(2)}) collective-permute-start(bf16[16,64,512]{2,1,0:T(8,128)(2,1)} %get-tuple-element.55), channel_id=1, source_target_pairs={{0,1},{1,0},{2,3},{3,2},{4,5},{5,4},{6,7},{7,6},{8,9},{9,8},{10,11... | collective-permute-start | bytes 3145736 | tf_op jit(solution)/shard_map/ppermute | solution.py:479
  799.5 15.0 %copy-start = (bf16[16,2,64,512]{3,2,1,0:T(8,128)(2,1)}, bf16[16,2,64,512]{3,2,1,0:T(8,128)(2,1)S(1)}, u32[]{:S(2)}) copy-start(bf16[16,2,64,512]{3,2,1,0:T(8,128)(2,1)S(1)} %all-to-all-done.8) | copy-start | bytes 6291460
  799.5 105.6 %all-to-all-start.10 = ((bf16[16,2,64,512]{3,2,1,0:T(8,128)(2,1)}), bf16[16,2,64,512]{3,2,1,0:T(8,128)(2,1)}, u32[]{:S(2)}, u32[]{:S(2)}) async-start(bf16[16,2,64,512]{3,2,1,0:T(8,128)(2,1)} %first.13), calls=%async_computation.10 | async-start | bytes 4194304 | tf_op jit(solution)/shard_map/all_to_all | solution.py:538
  832.7 24.5 %collective-permute-start.17 = (bf16[16,64,512]{2,1,0:T(8,128)(2,1)}, bf16[16,64,512]{2,1,0:T(8,128)(2,1)S(1)}, u32[]{:S(2)}, u32[]{:S(2)}) collective-permute-start(bf16[16,64,512]{2,1,0:T(8,128)(2,1)} %bitcast.186), channel_id=1, source_target_pairs={{0,1},{1,0},{2,3},{3,2},{4,5},{5,4},{6,7},{7,6},{8,9},{9,8},{10,11... | collective-permute-start | bytes 3145736 | tf_op jit(solution)/shard_map/ppermute | solution.py:479
  835.6 44.0 %collective-permute-start.5 = (bf16[16,64,512]{2,1,0:T(8,128)(2,1)S(1)}, bf16[16,64,512]{2,1,0:T(8,128)(2,1)S(1)}, u32[]{:S(2)}, u32[]{:S(2)}) collective-permute-start(bf16[16,64,512]{2,1,0:T(8,128)(2,1)S(1)} %get-tuple-element.128), channel_id=1, source_target_pairs={{0,1},{1,0},{2,3},{3,2},{4,5},{5,4},{6,7},{7,6},{8,9},{9,8},{10,11... | collective-permute-start | bytes 3145736 | tf_op jit(solution)/shard_map/ppermute | solution.py:479
  865.7 36.4 %collective-permute-start.18 = (bf16[16,64,512]{2,1,0:T(8,128)(2,1)}, bf16[16,64,512]{2,1,0:T(8,128)(2,1)S(1)}, u32[]{:S(2)}, u32[]{:S(2)}) collective-permute-start(bf16[16,64,512]{2,1,0:T(8,128)(2,1)} %get-tuple-element.79), channel_id=1, source_target_pairs={{0,1},{1,0},{2,3},{3,2},{4,5},{5,4},{6,7},{7,6},{8,9},{9,8},{10,11... | collective-permute-start | bytes 3145736 | tf_op jit(solution)/shard_map/ppermute | solution.py:479
  885.0 39.6 %collective-permute-start.6 = (bf16[16,64,512]{2,1,0:T(8,128)(2,1)}, bf16[16,64,512]{2,1,0:T(8,128)(2,1)S(1)}, u32[]{:S(2)}, u32[]{:S(2)}) collective-permute-start(bf16[16,64,512]{2,1,0:T(8,128)(2,1)} %get-tuple-element.53), channel_id=1, source_target_pairs={{0,1},{1,0},{2,3},{3,2},{4,5},{5,4},{6,7},{7,6},{8,9},{9,8},{10,11... | collective-permute-start | bytes 3145736 | tf_op jit(solution)/shard_map/ppermute | solution.py:479
  905.1 95.6 %all-to-all-start.11 = ((bf16[16,2,64,512]{3,2,1,0:T(8,128)(2,1)}), bf16[16,2,64,512]{3,2,1,0:T(8,128)(2,1)S(1)}, u32[]{:S(2)}, u32[]{:S(2)}) async-start(bf16[16,2,64,512]{3,2,1,0:T(8,128)(2,1)} %bitcast.69), calls=%async_computation.11 | async-start | bytes 4194304 | tf_op jit(solution)/shard_map/all_to_all | solution.py:538
  942.8 23.7 %collective-permute-start.19 = (bf16[16,64,512]{2,1,0:T(8,128)(2,1)}, bf16[16,64,512]{2,1,0:T(8,128)(2,1)S(1)}, u32[]{:S(2)}, u32[]{:S(2)}) collective-permute-start(bf16[16,64,512]{2,1,0:T(8,128)(2,1)} %bitcast.187), channel_id=1, source_target_pairs={{0,1},{1,0},{2,3},{3,2},{4,5},{5,4},{6,7},{7,6},{8,9},{9,8},{10,11... | collective-permute-start | bytes 3145736 | tf_op jit(solution)/shard_map/ppermute | solution.py:479
  975.0 22.8 %collective-permute-start.20 = (bf16[16,64,512]{2,1,0:T(8,128)(2,1)}, bf16[16,64,512]{2,1,0:T(8,128)(2,1)S(1)}, u32[]{:S(2)}, u32[]{:S(2)}) collective-permute-start(bf16[16,64,512]{2,1,0:T(8,128)(2,1)} %get-tuple-element.83), channel_id=1, source_target_pairs={{0,1},{1,0},{2,3},{3,2},{4,5},{5,4},{6,7},{7,6},{8,9},{9,8},{10,11... | collective-permute-start | bytes 3145736 | tf_op jit(solution)/shard_map/ppermute | solution.py:479
  1000.7 56.2 %all-to-all-start.13 = ((bf16[16,2,64,512]{3,2,1,0:T(8,128)(2,1)}), bf16[16,2,64,512]{3,2,1,0:T(8,128)(2,1)}, u32[]{:S(2)}, u32[]{:S(2)}) async-start(bf16[16,2,64,512]{3,2,1,0:T(8,128)(2,1)} %bitcast.73), calls=%async_computation.13 | async-start | bytes 4194304 | tf_op jit(solution)/shard_map/all_to_all | solution.py:538
  1056.9 52.2 %all-to-all-start.12 = ((bf16[16,2,64,512]{3,2,1,0:T(8,128)(2,1)}), bf16[16,2,64,512]{3,2,1,0:T(8,128)(2,1)S(1)}, u32[]{:S(2)}, u32[]{:S(2)}) async-start(bf16[16,2,64,512]{3,2,1,0:T(8,128)(2,1)} %first.14), calls=%async_computation.12 | async-start | bytes 4194304 | tf_op jit(solution)/shard_map/all_to_all | solution.py:538
  1109.1 29.0 %copy-start.1 = (bf16[16,2,64,512]{3,2,1,0:T(8,128)(2,1)}, bf16[16,2,64,512]{3,2,1,0:T(8,128)(2,1)S(1)}, u32[]{:S(2)}) copy-start(bf16[16,2,64,512]{3,2,1,0:T(8,128)(2,1)S(1)} %all-to-all-done.12) | copy-start | bytes 6291460
  1109.1 97.6 %all-to-all-start.14 = ((bf16[16,2,64,512]{3,2,1,0:T(8,128)(2,1)}), bf16[16,2,64,512]{3,2,1,0:T(8,128)(2,1)}, u32[]{:S(2)}, u32[]{:S(2)}) async-start(bf16[16,2,64,512]{3,2,1,0:T(8,128)(2,1)} %first.15), calls=%async_computation.14 | async-start | bytes 4194304 | tf_op jit(solution)/shard_map/all_to_all | solution.py:538
  1114.2 23.9 %copy-start.12 = (f32[16,128,32]{2,1,0:T(8,128)S(1)}, f32[16,128,32]{2,1,0:T(8,128)}, u32[]{:S(2)}) copy-start(f32[16,128,32]{2,1,0:T(8,128)} %get-tuple-element.85) | copy-start | bytes 786436
  1114.2 23.9 %copy-start.13 = (f32[16,128,32]{2,1,0:T(8,128)S(1)}, f32[16,128,32]{2,1,0:T(8,128)}, u32[]{:S(2)}) copy-start(f32[16,128,32]{2,1,0:T(8,128)} %get-tuple-element.86) | copy-start | bytes 786436
  1114.2 23.9 %copy-start.14 = (f32[16,128,32]{2,1,0:T(8,128)S(1)}, f32[16,128,32]{2,1,0:T(8,128)}, u32[]{:S(2)}) copy-start(f32[16,128,32]{2,1,0:T(8,128)} %get-tuple-element.87) | copy-start | bytes 786436
  1114.2 23.9 %copy-start.15 = (f32[16,128,32]{2,1,0:T(8,128)S(1)}, f32[16,128,32]{2,1,0:T(8,128)}, u32[]{:S(2)}) copy-start(f32[16,128,32]{2,1,0:T(8,128)} %get-tuple-element.88) | copy-start | bytes 786436
  1189.8 14.1 %copy-start.19 = (f32[2,1024,64]{2,1,0:T(8,128)S(1)}, f32[2,1024,64]{2,1,0:T(8,128)}, u32[]{:S(2)}) copy-start(f32[2,1024,64]{2,1,0:T(8,128)} %first_grad.4) | copy-start | bytes 1572868
  1189.8 14.1 %copy-start.20 = (f32[2,1024,64]{2,1,0:T(8,128)S(1)}, f32[2,1024,64]{2,1,0:T(8,128)}, u32[]{:S(2)}) copy-start(f32[2,1024,64]{2,1,0:T(8,128)} %first_grad.5) | copy-start | bytes 1572868
  1189.8 14.1 %copy-start.21 = (f32[2,1024,64]{2,1,0:T(8,128)S(1)}, f32[2,1024,64]{2,1,0:T(8,128)}, u32[]{:S(2)}) copy-start(f32[2,1024,64]{2,1,0:T(8,128)} %first_grad.7) | copy-start | bytes 1572868
  (24 other events, 75.2 us)
